TPU v7x, 768 devices: a whole 4x8x12 slice. The times are simulated.
768 devices in a mesh: dp: 192 (over z, x_hi, y), section: 4 (over x_lo, core).
Axes of the slice: x: 4 (x_hi: 2, x_lo: 2; x = x_hi * 2 + x_lo), y: 8, z: 12, core: 2. Of those that a mesh axis runs over, the one named last changes fastest.
Arguments:
- hidden_input_rows: bfloat16 [4, 24576, 3584], P('section', 'dp'), may hold values from -6 to 6
- embeddings: bfloat16 [4, 24576, 3584], P('section', 'dp'), may hold values from -6 to 6
- adapter_down_weight: bfloat16 [4, 2, 64, 7168], P('section'), may hold values from -0.0625 to 0.0625
- adapter_up_weight: bfloat16 [4, 2, 64, 3584], P('section'), may hold values from -0.75 to 0.75
- shared_norm_gain: float32 [2, 7168], replicated, may hold values from 0.1 to 1.9
- plan: int32 [4, 2], P('section'), may hold values from 0 to 2
- adapter_output_cotangent: bfloat16 [4, 24576, 3584], P('section', 'dp'), may hold values from -6 to 6
Outputs:
- carried_final_rows: bfloat16 [4, 24576, 3584], P('section', 'dp')
- lora_b_grad: float32 [4, 2, 64, 3584], P('section')
- gain_grad: float32 [2, 7168], replicated
Inputs may be any that keep to these rules, and one draw needn't show every extreme that they name: `plan`: an entry 2 means that the layer calls no shared block.
All inputs are finite; a program needn't handle non-finite values.
Results may differ from a plain program's by a relative error of at most 0.007.
Values may be sent and summed in bfloat16 or wider, within the bound.
No kernel may reach another device: no remote copies, remote signals or barrier semaphores. Data moves between devices by JAX's collectives and lax.ppermute only.
A program may use at most 64 MiB of HBM per device.

v0:
```python
import functools
import math

import jax
import jax.numpy as jnp
import numpy as np
from jax import lax
from jax.experimental import pallas as pl
from jax.experimental.pallas import tpu as pltpu
from jax.sharding import Mesh
from jax.sharding import PartitionSpec as P


F32 = jnp.float32
BF16 = jnp.bfloat16
STEP_LANES = 512
ID_LANES = 128
CONTRACT_LAST = (((1,), (1,)), ((), ()))
CONTRACT_FIRST = (((0,), (0,)), ((), ()))


def layer_kernel(own, hidden, embed, cot, gain, gain_total, *refs):
    width = hidden.shape[-1]
    if own:
        down_ref, up_ref, id_ref, state_out, grad_out, gain_out, scaled = refs

        def down(start, size):
            return down_ref[0, 0, :, start : start + size]

        def up(start, size):
            return up_ref[0, 0, :, start : start + size]

        ids = id_ref[...]
    else:
        first, second, state_out, grad_out, gain_out, scaled = refs

        def down(start, size):
            return jnp.concatenate(
                [first[:, start : start + size], second[:, start : start + size]], axis=0
            )

        def up(start, size):
            return down(2 * width + start, size)

        ids = first[0:1, 3 * width : 3 * width + ID_LANES].astype(F32)
    block_id = jnp.max(ids, axis=1, keepdims=True)
    pick_0 = (jnp.abs(block_id - 0.0) < 0.5).astype(F32)
    pick_1 = (jnp.abs(block_id - 1.0) < 0.5).astype(F32)
    active = pick_0 + pick_1

    starts = range(0, width, STEP_LANES)
    squares = jnp.zeros((hidden.shape[0], ID_LANES), F32)
    for rows in (hidden, embed):
        for start in starts:
            wide = rows[:, start : start + STEP_LANES].astype(F32)
            wide = wide * wide
            for lane in range(0, STEP_LANES, ID_LANES):
                squares = squares + wide[:, lane : lane + ID_LANES]
    squares_sum = jnp.sum(squares, axis=1, keepdims=True)
    inverse = lax.rsqrt(squares_sum / (2 * width) + 1e-05)

    latent_grad = lax.dot_general(
        cot[...], up(0, width), CONTRACT_LAST, preferred_element_type=F32
    ).astype(BF16)
    for part, rows in enumerate((hidden, embed)):
        for start in starts:
            here = part * width + start
            lanes = slice(here, here + STEP_LANES)
            normed = rows[:, start : start + STEP_LANES].astype(F32) * inverse
            gain_now = pick_0 * gain[0:1, lanes] + pick_1 * gain[1:2, lanes]
            scaled[:, lanes] = (normed * gain_now).astype(BF16)
            normed_grad = jnp.dot(
                latent_grad, down(here, STEP_LANES), preferred_element_type=F32
            )
            piece = jnp.sum(normed_grad * normed, axis=0, keepdims=True)
            gain_out[0:1, lanes] = gain_total[0:1, lanes] + pick_0 * piece
            gain_out[1:2, lanes] = gain_total[1:2, lanes] + pick_1 * piece
    latent = lax.dot_general(
        scaled[...], down(0, 2 * width), CONTRACT_LAST, preferred_element_type=F32
    ).astype(BF16)
    for start in starts:
        lanes = slice(start, start + STEP_LANES)
        update = jnp.dot(latent, up(start, STEP_LANES), preferred_element_type=F32)
        wide = hidden[:, lanes].astype(F32)
        state_out[:, lanes] = jnp.where(active > 0.5, wide + update, wide).astype(BF16)
        grad = lax.dot_general(
            latent, cot[:, lanes], CONTRACT_FIRST, preferred_element_type=F32
        )
        grad_out[:, lanes] = (active * grad).astype(BF16)


def layer(own, hidden, embed, cot, gain, gain_total, *weights):
    rows, width = hidden.shape
    rank = weights[0].shape[2] if own else 2 * weights[0].shape[0]
    return pl.pallas_call(
        functools.partial(layer_kernel, own),
        out_shape=(
            jax.ShapeDtypeStruct((rows, width), BF16),
            jax.ShapeDtypeStruct((rank, width), BF16),
            jax.ShapeDtypeStruct(gain.shape, F32),
        ),
        scratch_shapes=[pltpu.VMEM((rows, 2 * width), BF16)],
        name="layer_own" if own else "layer_sent",
    )(hidden, embed, cot, gain, gain_total, *weights)


def pack_kernel(slot, down, up, ids, *packets):
    width, half = up.shape[-1], packets[0].shape[0]
    here = slot[0]
    block_id = jnp.where(here == 0, ids[0], ids[1])
    for side, packet in enumerate(packets):
        rows = slice(side * half, (side + 1) * half)
        packet[:, : 2 * width] = down[0, 0, rows, :]
        packet[:, 2 * width : 3 * width] = up[0, 0, rows, :]
        packet[:, 3 * width :] = jnp.full((half, ID_LANES), block_id, F32).astype(BF16)


def pack(slot, down, up, ids):
    rank, width = up.shape[2:]
    half = rank // 2
    packet = jax.ShapeDtypeStruct((half, 3 * width + ID_LANES), BF16)
    whole = pl.BlockSpec(packet.shape, lambda i, slot: (0, 0))
    return pl.pallas_call(
        pack_kernel,
        out_shape=(packet, packet),
        grid_spec=pltpu.PrefetchScalarGridSpec(
            num_scalar_prefetch=1,
            grid=(1,),
            in_specs=[
                pl.BlockSpec((1, 1, rank, 2 * width), lambda i, slot: (0, slot[0], 0, 0)),
                pl.BlockSpec((1, 1, rank, width), lambda i, slot: (0, slot[0], 0, 0)),
                pl.BlockSpec(memory_space=pltpu.SMEM),
            ],
            out_specs=(whole, whole),
        ),
        name="pack",
    )(slot, down, up, ids)


def exchange(array, axes):
    return lax.all_to_all(array, axes, 0, 0)


def everyone(array, axes, count):
    return exchange(jnp.broadcast_to(array[None], (count,) + array.shape), axes)


def two_parts(wide):
    high = lax.reduce_precision(wide, 8, 7)
    return high, wide - high


def on_device(
    n_xh, n_y, n_z, n_xl, n_core, hidden_input_rows, embeddings, down, up, gain, plan, cotangent
):
    sections = n_xl * n_core
    position = lax.axis_index("xl") * n_core + lax.axis_index("core")
    hidden, embed, cot = hidden_input_rows[0], embeddings[0], cotangent[0]
    rows, width = hidden.shape
    slots, rank = down.shape[1], down.shape[2]
    ring = ("xh", "xl", "core")

    def weights_route(shift, side):
        route = []
        for xh in range(n_xh):
            for s in range(sections):
                source = (s + shift) % sections
                other = side and source // n_core != s // n_core
                from_xh = (xh + 1) % n_xh if other else xh
                route.append((from_xh * sections + source, xh * sections + s))
        return route

    def section_route(shift):
        return [
            (xh * sections + s, xh * sections + (s + shift) % sections)
            for xh in range(n_xh)
            for s in range(sections)
        ]

    ids = plan[0].astype(F32)
    arrived = []
    for shift in range(1, sections):
        slot = (position < shift).astype(jnp.int32).reshape(1)
        packets = pack(slot, down, up, ids)
        sides = []
        for side in range(2):
            sides.append(lax.ppermute(packets[side], ring, weights_route(shift, side)))
        arrived.append(sides)

    own_id = jnp.broadcast_to(ids[0], (1, ID_LANES))
    state, grad, gain_total = layer(
        True, hidden, embed, cot, gain, jnp.zeros(gain.shape, F32), down, up, own_id
    )
    wide = grad.astype(F32)
    totals = [wide, jnp.zeros_like(wide)]
    sent = []
    for shift in range(1, sections):
        state, grad, gain_total = layer(
            False, state, embed, cot, gain, gain_total, *arrived[shift - 1]
        )
        sent.append(lax.ppermute(grad, ring, section_route(shift)))
    gain_total = jnp.sum(everyone(gain_total, ("xl", "core"), sections), axis=0)
    final_rows = lax.ppermute(state, ring, section_route(-1))
    for shift, grad in enumerate(sent, 1):
        late = position < shift
        wide = grad.astype(F32)
        totals[0] = totals[0] + jnp.where(late, 0.0, wide)
        totals[1] = totals[1] + jnp.where(late, wide, 0.0)

    near = n_xh * n_y
    deep = slots * rank // near
    gain_lanes = gain.size // (near * deep)
    room = -(-gain_lanes // 128) * 128
    lanes = width + 2 * room
    grads = jnp.stack(totals).reshape(near, deep, width)

    def with_gain(grads, gains):
        pad = [(0, 0)] * (gains.ndim - 1) + [(0, room - gains.shape[-1])]
        parts = [jnp.pad(x, pad) for x in two_parts(gains)]
        return jnp.concatenate([grads] + parts, axis=-1).astype(BF16)

    packet = with_gain(grads, gain_total.reshape(near, deep, gain_lanes))
    packet = exchange(packet, ("xh", "y"))
    total = jnp.sum(packet.astype(F32), axis=0)
    packet = with_gain(
        total[:, :width], total[:, width : width + room] + total[:, width + room :]
    )
    packet = packet.reshape(n_z, deep * lanes // 128 // n_z, 128)
    packet = exchange(packet, "z")
    total = jnp.sum(packet.astype(F32), axis=0).astype(BF16)
    total = everyone(total, "z", n_z)
    total = total.reshape(deep, lanes)
    total = everyone(total, ("xh", "y"), near)
    total = total.astype(F32)
    scale = 1.0 / math.sqrt(rows * n_xh * n_y * n_z)
    lora = (total[:, :, :width] * scale).reshape(1, slots, rank, width)
    gains = total[:, :, width : width + gain_lanes]
    gains = gains + total[:, :, width + room : width + room + gain_lanes]
    return final_rows[None], lora, (gains * scale).reshape(gain.shape)


def solution(mesh):
    n_dp, sections = mesh.devices.shape
    n_z, n_xh, n_xl = 12, 2, 2
    n_y, n_core = n_dp // (n_z * n_xh), sections // n_xl
    fine = Mesh(
        np.asarray(mesh.devices).reshape(n_z, n_xh, n_y, n_xl, n_core),
        ("z", "xh", "y", "xl", "core"),
    )
    dp, section = ("z", "xh", "y"), ("xl", "core")
    rows = P(section, dp, None)
    weights = P(section, None, None, None)
    return jax.shard_map(
        functools.partial(on_device, n_xh, n_y, n_z, n_xl, n_core),
        mesh=fine,
        in_specs=(rows, rows, weights, weights, P(), P(section, None), rows),
        out_specs=(rows, weights, P()),
        check_vma=False,
    )
```

profile of v0, /device:TPU:8, one launch (start us, length us, event | category | flops | bytes accessed | tf_op | source)
XLA Modules:
  0.0 194.3 jit_solution(16039923859902946988)
XLA Ops:
  0.6 1.2 convert_bitcast_fusion
  1.8 2.4 %pack.3 = (bf16[32,10880]{1,0:T(8,128)(2,1)}, bf16[32,10880]{1,0:T(8,128)(2,1)}) custom-call(s32[1]{0:T(128)} %bitcast.4.slot, bf16[1,2,64,7168]{3,2,1,0:T(8,128)(2,1)} %down.5, bf16[1,2,64,3584]{3,2,1,0:T(8,128)(2,1)} %up.5, f32[2]{0:T(128)} %get-tuple-element.45.ids), custom_call_target="tpu_custom_call" | custom-call | tf_op jit(solution)/shard_map/pack/pallas_call | solution.py:123
  4.2 2.8 %collective-permute-start = (bf16[32,10880]{1,0:T(8,128)(2,1)}, bf16[32,10880]{1,0:T(8,128)(2,1)S(1)}, u32[]{:S(2)}, u32[]{:S(2)}) collective-permute-start(bf16[32,10880]{1,0:T(8,128)(2,1)} %get-tuple-element.23), channel_id=1, source_target_pairs={{1,0},{2,1},{3,2},{0,3},{33,32},{34,33},{35,34},{32,35},{5,4},{6,5... | collective-permute-start | bytes 2088968 | tf_op jit(solution)/shard_map/ppermute | solution.py:187
  7.1 3.9 %collective-permute-start.1 = (bf16[32,10880]{1,0:T(8,128)(2,1)}, bf16[32,10880]{1,0:T(8,128)(2,1)S(1)}, u32[]{:S(2)}, u32[]{:S(2)}) collective-permute-start(bf16[32,10880]{1,0:T(8,128)(2,1)} %get-tuple-element.24), channel_id=1, source_target_pairs={{1,0},{34,1},{3,2},{32,3},{33,32},{2,33},{35,34},{0,35},{5,4},{38,... | collective-permute-start | bytes 2088968 | tf_op jit(solution)/shard_map/ppermute | solution.py:187
  10.9 2.4 %pack.4 = (bf16[32,10880]{1,0:T(8,128)(2,1)}, bf16[32,10880]{1,0:T(8,128)(2,1)}) custom-call(s32[1]{0:T(128)} %bitcast.6.slot, bf16[1,2,64,7168]{3,2,1,0:T(8,128)(2,1)} %down.5, bf16[1,2,64,3584]{3,2,1,0:T(8,128)(2,1)} %up.5, f32[2]{0:T(128)} %get-tuple-element.45.ids), custom_call_target="tpu_custom_call" | custom-call | tf_op jit(solution)/shard_map/pack/pallas_call | solution.py:123
  13.4 2.1 %collective-permute-start.2 = (bf16[32,10880]{1,0:T(8,128)(2,1)}, bf16[32,10880]{1,0:T(8,128)(2,1)S(1)}, u32[]{:S(2)}, u32[]{:S(2)}) collective-permute-start(bf16[32,10880]{1,0:T(8,128)(2,1)} %get-tuple-element.27), channel_id=1, source_target_pairs={{2,0},{3,1},{0,2},{1,3},{34,32},{35,33},{32,34},{33,35},{6,4},{7,5... | collective-permute-start | bytes 2088968 | tf_op jit(solution)/shard_map/ppermute | solution.py:187
  15.5 3.0 %collective-permute-start.3 = (bf16[32,10880]{1,0:T(8,128)(2,1)}, bf16[32,10880]{1,0:T(8,128)(2,1)S(1)}, u32[]{:S(2)}, u32[]{:S(2)}) collective-permute-start(bf16[32,10880]{1,0:T(8,128)(2,1)} %get-tuple-element.28), channel_id=1, source_target_pairs={{34,0},{35,1},{32,2},{33,3},{2,32},{3,33},{0,34},{1,35},{38,4},{39... | collective-permute-start | bytes 2088968 | tf_op jit(solution)/shard_map/ppermute | solution.py:187
  18.6 2.5 %pack.5 = (bf16[32,10880]{1,0:T(8,128)(2,1)}, bf16[32,10880]{1,0:T(8,128)(2,1)}) custom-call(s32[1]{0:T(128)} %bitcast.7.slot, bf16[1,2,64,7168]{3,2,1,0:T(8,128)(2,1)} %down.5, bf16[1,2,64,3584]{3,2,1,0:T(8,128)(2,1)} %up.5, f32[2]{0:T(128)} %get-tuple-element.45.ids), custom_call_target="tpu_custom_call" | custom-call | tf_op jit(solution)/shard_map/pack/pallas_call | solution.py:123
  21.0 1.9 collective-permute-start.4
  22.9 0.0 collective-permute-done.refs_0_
  23.0 2.7 %collective-permute-start.5 = (bf16[32,10880]{1,0:T(8,128)(2,1)}, bf16[32,10880]{1,0:T(8,128)(2,1)}, u32[]{:S(2)}, u32[]{:S(2)}) collective-permute-start(bf16[32,10880]{1,0:T(8,128)(2,1)} %get-tuple-element.32), channel_id=1, source_target_pairs={{35,0},{0,1},{33,2},{2,3},{3,32},{32,33},{1,34},{34,35},{39,4},{4,... | collective-permute-start | bytes 2088968 | tf_op jit(solution)/shard_map/ppermute | solution.py:187
  25.7 0.6 broadcast_in_dim.39.refs_2_
  26.3 0.6 broadcast_in_dim.38.gain_total
  26.9 7.0 %layer_own.1 = (bf16[128,3584]{1,0:T(8,128)(2,1)}, bf16[64,3584]{1,0:T(8,128)(2,1)}, f32[2,7168]{1,0:T(2,128)}) custom-call(bf16[128,3584]{1,0:T(8,128)(2,1)} %bitcast.28, bf16[128,3584]{1,0:T(8,128)(2,1)} %bitcast.17, bf16[128,3584]{1,0:T(8,128)(2,1)} %bitcast.21, f32[2,7168]{1,0:T(2,128)} %gain.7, f32[2,7168]{1,0:T(2,128)} %broadcast_in_dim.38.gain_total, ...), custom_call_target="tpu_custom_call" | custom-call | tf_op jit(solution)/shard_map/layer_own/pallas_call | solution.py:95
  34.0 0.0 collective-permute-done.1.refs_1_
  34.0 0.9 copy-done.3
  34.8 6.5 %layer_sent.3 = (bf16[128,3584]{1,0:T(8,128)(2,1)}, bf16[64,3584]{1,0:T(8,128)(2,1)}, f32[2,7168]{1,0:T(2,128)}) custom-call(bf16[128,3584]{1,0:T(8,128)(2,1)} %get-tuple-element.21.hidden, bf16[128,3584]{1,0:T(8,128)(2,1)} %bitcast.18, bf16[128,3584]{1,0:T(8,128)(2,1)} %bitcast.22, f32[2,7168]{1,0:T(2,128)} %gain.7, ...), custom_call_target="tpu_custom_call" | custom-call | tf_op jit(solution)/shard_map/layer_sent/pallas_call | solution.py:95
  41.4 0.8 copy-done.1
  42.2 0.2 copy-done.4
  42.5 6.6 %layer_sent.4 = (bf16[128,3584]{1,0:T(8,128)(2,1)}, bf16[64,3584]{1,0:T(8,128)(2,1)}, f32[2,7168]{1,0:T(2,128)}) custom-call(bf16[128,3584]{1,0:T(8,128)(2,1)} %get-tuple-element.25.hidden, bf16[128,3584]{1,0:T(8,128)(2,1)} %bitcast.19, bf16[128,3584]{1,0:T(8,128)(2,1)} %bitcast.23, f32[2,7168]{1,0:T(2,128)} %gain.7, ...), custom_call_target="tpu_custom_call" | custom-call | tf_op jit(solution)/shard_map/layer_sent/pallas_call | solution.py:95
  49.0 0.0 collective-permute-done.4.refs_0_
  49.0 0.8 copy-done.2
  49.9 6.6 %layer_sent.5 = (bf16[128,3584]{1,0:T(8,128)(2,1)}, bf16[64,3584]{1,0:T(8,128)(2,1)}, f32[2,7168]{1,0:T(2,128)}) custom-call(bf16[128,3584]{1,0:T(8,128)(2,1)} %get-tuple-element.29.hidden, bf16[128,3584]{1,0:T(8,128)(2,1)} %bitcast.20, bf16[128,3584]{1,0:T(8,128)(2,1)} %bitcast.24, f32[2,7168]{1,0:T(2,128)} %gain.7, ...), custom_call_target="tpu_custom_call" | custom-call | tf_op jit(solution)/shard_map/layer_sent/pallas_call | solution.py:95
  56.5 3.5 %collective-permute-start.9 = (bf16[64,3584]{1,0:T(8,128)(2,1)}, bf16[64,3584]{1,0:T(8,128)(2,1)S(1)}, u32[]{:S(2)}, u32[]{:S(2)}) collective-permute-start(bf16[64,3584]{1,0:T(8,128)(2,1)} %get-tuple-element.37), channel_id=1, source_target_pairs={{0,3},{1,0},{2,1},{3,2},{32,35},{33,32},{34,33},{35,34},{4,7},{5,4... | collective-permute-start | bytes 1376264 | tf_op jit(solution)/shard_map/ppermute | solution.py:201
  60.1 3.5 %collective-permute-start.8 = (bf16[64,3584]{1,0:T(8,128)(2,1)}, bf16[64,3584]{1,0:T(8,128)(2,1)S(1)}, u32[]{:S(2)}, u32[]{:S(2)}) collective-permute-start(bf16[64,3584]{1,0:T(8,128)(2,1)} %get-tuple-element.36), channel_id=1, source_target_pairs={{0,2},{1,3},{2,0},{3,1},{32,34},{33,35},{34,32},{35,33},{4,6},{5,7... | collective-permute-start | bytes 1376264 | tf_op jit(solution)/shard_map/ppermute | solution.py:201
  63.6 1.9 collective-permute-start.7
  65.5 0.9 broadcast_in_dim.42
  66.4 18.7 %all_to_all.25 = f32[4,2,7168]{2,1,0:T(2,128)S(1)} all-to-all(f32[4,2,7168]{2,1,0:T(2,128)S(1)} %broadcast_in_dim.42), channel_id=1, replica_groups=mesh['z'=12,'xh'=2,'y'=8,'xl'=2,'core'=2] {'xl','core'}, dimensions={0} | all-to-all | bytes 458752 | tf_op jit(solution)/shard_map/all_to_all | solution.py:141
  85.1 0.1 reduce_sum.30
  85.2 0.1 reshape.50
  85.4 0.5 fusion.13
  85.8 0.1 pad_maximum_fusion
  85.9 0.1 fusion.4
  86.0 37.7 %all_to_all.26 = bf16[16,8,3840]{2,1,0:T(8,128)(2,1)S(1)} all-to-all(bf16[16,8,3840]{2,1,0:T(8,128)(2,1)S(1)} %fusion.4), channel_id=1, replica_groups=mesh['z'=12,'xh'=2,'y'=8,'xl'=2,'core'=2] {'xh','y'}, dimensions={0} | all-to-all | bytes 1966080 | tf_op jit(solution)/shard_map/all_to_all | solution.py:141
  123.7 0.1 convert_reduce_fusion
  123.9 0.1 convert_element_type.44
  124.0 23.2 %all_to_all.27 = bf16[12,20,128]{2,1,0:T(8,128)(2,1)S(1)} all-to-all(bf16[12,20,128]{2,1,0:T(8,128)(2,1)S(1)} %convert_element_type.44), channel_id=1, replica_groups=mesh['z'=12,'xh'=2,'y'=8,'xl'=2,'core'=2] {'z'}, dimensions={0} | all-to-all | bytes 122880 | tf_op jit(solution)/shard_map/all_to_all | solution.py:141
  147.2 13.8 %all_to_all.28 = bf16[12,20,128]{2,1,0:T(8,128)(2,1)S(1)} all-to-all(bf16[12,20,128]{2,1,0:T(8,128)(2,1)S(1)} %broadcast_in_dim.43), channel_id=1, replica_groups=mesh['z'=12,'xh'=2,'y'=8,'xl'=2,'core'=2] {'z'}, dimensions={0} | all-to-all | bytes 122880 | tf_op jit(solution)/shard_map/all_to_all | solution.py:141
  161.0 0.1 broadcast_in_dim.44
  161.1 1.0 broadcast_in_dim.45
  162.1 5.5 %all-to-all-start.4 = ((bf16[16,8,3840]{2,1,0:T(8,128)(2,1)}), bf16[16,8,3840]{2,1,0:T(8,128)(2,1)S(1)}, u32[]{:S(2)}, u32[]{:S(2)}) async-start(bf16[16,8,3840]{2,1,0:T(8,128)(2,1)} %broadcast_in_dim.45), calls=%async_computation.4 | async-start | bytes 1966080 | tf_op jit(solution)/shard_map/all_to_all | solution.py:141
  167.6 1.9 collective-permute-start.6
  169.6 18.5 %collective-permute-done.6 = bf16[128,3584]{1,0:T(8,128)(2,1)S(1)} collective-permute-done((bf16[128,3584]{1,0:T(8,128)(2,1)S(1)}, bf16[128,3584]{1,0:T(8,128)(2,1)S(1)}, u32[]{:S(2)}, u32[]{:S(2)}) %collective-permute-start.6) | collective-permute-done | bytes 917536 | tf_op jit(solution)/shard_map/ppermute | solution.py:203
  188.1 2.9 %all-to-all-done.4 = bf16[16,8,3840]{2,1,0:T(8,128)(2,1)S(1)} async-done(((bf16[16,8,3840]{2,1,0:T(8,128)(2,1)}), bf16[16,8,3840]{2,1,0:T(8,128)(2,1)S(1)}, u32[]{:S(2)}, u32[]{:S(2)}) %all-to-all-start.4) | async-done | bytes 983072 | tf_op jit(solution)/shard_map/all_to_all | solution.py:141
  191.0 0.1 convert_element_type.45
  191.1 1.5 slice_multiply_fusion
  192.6 0.8 reshape.52
  193.3 0.9 copy.13
  (25 shorter events, 0.1 us)
Async XLA Ops:
  4.2 18.7 %collective-permute-start = (bf16[32,10880]{1,0:T(8,128)(2,1)}, bf16[32,10880]{1,0:T(8,128)(2,1)S(1)}, u32[]{:S(2)}, u32[]{:S(2)}) collective-permute-start(bf16[32,10880]{1,0:T(8,128)(2,1)} %get-tuple-element.23), channel_id=1, source_target_pairs={{1,0},{2,1},{3,2},{0,3},{33,32},{34,33},{35,34},{32,35},{5,4},{6,5... | collective-permute-start | bytes 2088968 | tf_op jit(solution)/shard_map/ppermute | solution.py:187
  7.1 26.9 %collective-permute-start.1 = (bf16[32,10880]{1,0:T(8,128)(2,1)}, bf16[32,10880]{1,0:T(8,128)(2,1)S(1)}, u32[]{:S(2)}, u32[]{:S(2)}) collective-permute-start(bf16[32,10880]{1,0:T(8,128)(2,1)} %get-tuple-element.24), channel_id=1, source_target_pairs={{1,0},{34,1},{3,2},{32,3},{33,32},{2,33},{35,34},{0,35},{5,4},{38,... | collective-permute-start | bytes 2088968 | tf_op jit(solution)/shard_map/ppermute | solution.py:187
  13.4 28.0 %collective-permute-start.2 = (bf16[32,10880]{1,0:T(8,128)(2,1)}, bf16[32,10880]{1,0:T(8,128)(2,1)S(1)}, u32[]{:S(2)}, u32[]{:S(2)}) collective-permute-start(bf16[32,10880]{1,0:T(8,128)(2,1)} %get-tuple-element.27), channel_id=1, source_target_pairs={{2,0},{3,1},{0,2},{1,3},{34,32},{35,33},{32,34},{33,35},{6,4},{7,5... | collective-permute-start | bytes 2088968 | tf_op jit(solution)/shard_map/ppermute | solution.py:187
  15.5 25.9 %collective-permute-start.3 = (bf16[32,10880]{1,0:T(8,128)(2,1)}, bf16[32,10880]{1,0:T(8,128)(2,1)S(1)}, u32[]{:S(2)}, u32[]{:S(2)}) collective-permute-start(bf16[32,10880]{1,0:T(8,128)(2,1)} %get-tuple-element.28), channel_id=1, source_target_pairs={{34,0},{35,1},{32,2},{33,3},{2,32},{3,33},{0,34},{1,35},{38,4},{39... | collective-permute-start | bytes 2088968 | tf_op jit(solution)/shard_map/ppermute | solution.py:187
  21.0 28.0 %collective-permute-start.4 = (bf16[32,10880]{1,0:T(8,128)(2,1)}, bf16[32,10880]{1,0:T(8,128)(2,1)S(1)}, u32[]{:S(2)}, u32[]{:S(2)}) collective-permute-start(bf16[32,10880]{1,0:T(8,128)(2,1)} %get-tuple-element.31), channel_id=1, source_target_pairs={{3,0},{0,1},{1,2},{2,3},{35,32},{32,33},{33,34},{34,35},{7,4},{4,5... | collective-permute-start | bytes 2088968 | tf_op jit(solution)/shard_map/ppermute | solution.py:187
  23.0 11.0 %copy-start = (bf16[32,10880]{1,0:T(8,128)(2,1)}, bf16[32,10880]{1,0:T(8,128)(2,1)S(1)}, u32[]{:S(2)}) copy-start(bf16[32,10880]{1,0:T(8,128)(2,1)S(1)} %collective-permute-done.refs_0_) | copy-start | bytes 2088964
  23.0 26.1 %collective-permute-start.5 = (bf16[32,10880]{1,0:T(8,128)(2,1)}, bf16[32,10880]{1,0:T(8,128)(2,1)}, u32[]{:S(2)}, u32[]{:S(2)}) collective-permute-start(bf16[32,10880]{1,0:T(8,128)(2,1)} %get-tuple-element.32), channel_id=1, source_target_pairs={{35,0},{0,1},{33,2},{2,3},{3,32},{32,33},{1,34},{34,35},{39,4},{4,... | collective-permute-start | bytes 2088968 | tf_op jit(solution)/shard_map/ppermute | solution.py:187
  34.0 0.9 copy-start.3
  41.4 0.9 copy-start.1
  41.4 1.1 copy-start.4
  49.0 0.9 copy-start.2
  49.9 13.7 %copy-start.7 = (bf16[64,3584]{1,0:T(8,128)(2,1)S(1)}, bf16[64,3584]{1,0:T(8,128)(2,1)}, u32[]{:S(2)}) copy-start(bf16[64,3584]{1,0:T(8,128)(2,1)} %get-tuple-element.35) | copy-start | bytes 1376260
  49.9 35.5 %copy-start.5 = (bf16[64,3584]{1,0:T(8,128)(2,1)S(1)}, bf16[64,3584]{1,0:T(8,128)(2,1)}, u32[]{:S(2)}) copy-start(bf16[64,3584]{1,0:T(8,128)(2,1)} %get-tuple-element.34) | copy-start | bytes 1376260
  56.5 28.8 %collective-permute-start.9 = (bf16[64,3584]{1,0:T(8,128)(2,1)}, bf16[64,3584]{1,0:T(8,128)(2,1)S(1)}, u32[]{:S(2)}, u32[]{:S(2)}) collective-permute-start(bf16[64,3584]{1,0:T(8,128)(2,1)} %get-tuple-element.37), channel_id=1, source_target_pairs={{0,3},{1,0},{2,1},{3,2},{32,35},{33,32},{34,33},{35,34},{4,7},{5,4... | collective-permute-start | bytes 1376264 | tf_op jit(solution)/shard_map/ppermute | solution.py:201
  60.1 25.3 %collective-permute-start.8 = (bf16[64,3584]{1,0:T(8,128)(2,1)}, bf16[64,3584]{1,0:T(8,128)(2,1)S(1)}, u32[]{:S(2)}, u32[]{:S(2)}) collective-permute-start(bf16[64,3584]{1,0:T(8,128)(2,1)} %get-tuple-element.36), channel_id=1, source_target_pairs={{0,2},{1,3},{2,0},{3,1},{32,34},{33,35},{34,32},{35,33},{4,6},{5,7... | collective-permute-start | bytes 1376264 | tf_op jit(solution)/shard_map/ppermute | solution.py:201
  63.6 21.7 %collective-permute-start.7 = (bf16[64,3584]{1,0:T(8,128)(2,1)S(1)}, bf16[64,3584]{1,0:T(8,128)(2,1)S(1)}, u32[]{:S(2)}, u32[]{:S(2)}) collective-permute-start(bf16[64,3584]{1,0:T(8,128)(2,1)S(1)} %copy-done.7), channel_id=1, source_target_pairs={{0,1},{1,2},{2,3},{3,0},{32,33},{33,34},{34,35},{35,32},{4,5},{5,6... | collective-permute-start | bytes 1376264 | tf_op jit(solution)/shard_map/ppermute | solution.py:201
  123.8 43.8 %copy-start.6 = (bf16[128,3584]{1,0:T(8,128)(2,1)S(1)}, bf16[128,3584]{1,0:T(8,128)(2,1)}, u32[]{:S(2)}) copy-start(bf16[128,3584]{1,0:T(8,128)(2,1)} %get-tuple-element.33) | copy-start | bytes 2752516
  162.1 28.8 %all-to-all-start.4 = ((bf16[16,8,3840]{2,1,0:T(8,128)(2,1)}), bf16[16,8,3840]{2,1,0:T(8,128)(2,1)S(1)}, u32[]{:S(2)}, u32[]{:S(2)}) async-start(bf16[16,8,3840]{2,1,0:T(8,128)(2,1)} %broadcast_in_dim.45), calls=%async_computation.4 | async-start | bytes 1966080 | tf_op jit(solution)/shard_map/all_to_all | solution.py:141
  167.6 20.4 %collective-permute-start.6 = (bf16[128,3584]{1,0:T(8,128)(2,1)S(1)}, bf16[128,3584]{1,0:T(8,128)(2,1)S(1)}, u32[]{:S(2)}, u32[]{:S(2)}) collective-permute-start(bf16[128,3584]{1,0:T(8,128)(2,1)S(1)} %copy-done.6), channel_id=1, source_target_pairs={{0,3},{1,0},{2,1},{3,2},{32,35},{33,32},{34,33},{35,34},{4,7},{5,4... | collective-permute-start | bytes 2752520 | tf_op jit(solution)/shard_map/ppermute | solution.py:203
where the time goes:
time: 195 us; the launch traced here: 194 us
  blocking collectives  93.3 us (48%)
  Pallas kernels  34.1 us (17%)
  starting transfers between devices  32.8 us (17%)
  waiting for transfers between devices  21.4 us (11%)
  local copies, waits for them, and re-layouts  7.95 us (4%)
  other arithmetic  3.67 us (2%)
    all_to_all x4, blocking collectives, exchange(): return lax.all_to_all(array, axes, 0, 0)  93.3 us
    pallas_call x4, Pallas kernels, layer(): pl.pallas_call(functools.partial(layer_kernel, own), out_shape=(jax.Shape...  26.8 us
    ppermute x1, waiting for transfers between devices, on_device(): final_rows = lax.ppermute(state, ring, section_route(-1))  18.5 us
    ppermute x6, starting transfers between devices, on_device(): sides.append(lax.ppermute(packets[side], ring, weights_route(shift, side)))  16.4 us
    ppermute x3, starting transfers between devices, on_device(): sent.append(lax.ppermute(grad, ring, section_route(shift)))  8.97 us
    pallas_call x3, Pallas kernels, pack(): pl.pallas_call(pack_kernel, out_shape=(packet, packet), grid_spec=pltpu.P...  7.33 us
    all_to_all x1, starting transfers between devices, exchange(): return lax.all_to_all(array, axes, 0, 0)  5.49 us
  transfers between devices with their start and end apart: 11, of which 2 were waited for; matrix products, arithmetic and copies ran while one was open for 1% of the time, Pallas kernels for 13%

commit v1 on v0

v1 whole, which is shorter than its diff:
```python
import functools
import math

import jax
import jax.numpy as jnp
import numpy as np
from jax import lax
from jax.experimental import pallas as pl
from jax.experimental.pallas import tpu as pltpu
from jax.sharding import Mesh
from jax.sharding import PartitionSpec as P


F32 = jnp.float32
BF16 = jnp.bfloat16
STEP_LANES = 512
ID_LANES = 128
CONTRACT_LAST = (((1,), (1,)), ((), ()))
CONTRACT_FIRST = (((0,), (0,)), ((), ()))


def layer_kernel(own, *refs):
    if own:
        plan, hidden_in, embed_in, cot_in, gain, down_in, up_in = refs[:7]
        rest = refs[7:]
        gain_total = None
    else:
        hidden_in, embed_in, cot_in, gain, gain_total, first, second = refs[:7]
        rest = refs[7:]
    state_out, grad_out, gain_out, hidden, embed, cot, down, up, ids, scaled, sems = rest
    rows, width = hidden.shape
    half = down.shape[0] // 2
    moves = [(hidden_in, hidden), (embed_in, embed), (cot_in, cot)]
    if own:
        moves += [(up_in.at[0, 0], up), (down_in.at[0, 0], down)]
    else:
        for side, packet in enumerate((first, second)):
            part = pl.ds(side * half, half)
            moves.append((packet.at[:, pl.ds(2 * width, width)], up.at[part]))
        moves.append((first.at[:, pl.ds(3 * width, ID_LANES)], ids))
        for side, packet in enumerate((first, second)):
            part = pl.ds(side * half, half)
            moves.append((packet.at[:, pl.ds(0, 2 * width)], down.at[part]))
    copies = [
        pltpu.make_async_copy(source, target, sems.at[i])
        for i, (source, target) in enumerate(moves)
    ]
    for copy in copies:
        copy.start()

    starts = range(0, width, STEP_LANES)
    squares = jnp.zeros((rows, ID_LANES), F32)
    for copy, source in zip(copies[:2], (hidden, embed)):
        copy.wait()
        for start in starts:
            wide = source[:, start : start + STEP_LANES].astype(F32)
            wide = wide * wide
            for lane in range(0, STEP_LANES, ID_LANES):
                squares = squares + wide[:, lane : lane + ID_LANES]
    squares_sum = jnp.sum(squares, axis=1, keepdims=True)
    inverse = lax.rsqrt(squares_sum / (2 * width) + 1e-05)

    for copy in copies[2 : 4 if own else 6]:
        copy.wait()
    if own:
        block_id = jnp.full((1, 1), plan[0, 0], jnp.int32).astype(F32)
    else:
        block_id = jnp.max(ids[0:1, :].astype(F32), axis=1, keepdims=True)
    pick_0 = (jnp.abs(block_id - 0.0) < 0.5).astype(F32)
    pick_1 = (jnp.abs(block_id - 1.0) < 0.5).astype(F32)
    active = pick_0 + pick_1
    latent_grad = lax.dot_general(
        cot[...], up[...], CONTRACT_LAST, preferred_element_type=F32
    ).astype(BF16)
    for copy in copies[4 if own else 6 :]:
        copy.wait()
    for part, source in enumerate((hidden, embed)):
        for start in starts:
            here = part * width + start
            lanes = slice(here, here + STEP_LANES)
            normed = source[:, start : start + STEP_LANES].astype(F32) * inverse
            gain_now = pick_0 * gain[0:1, lanes] + pick_1 * gain[1:2, lanes]
            scaled[:, lanes] = (normed * gain_now).astype(BF16)
            normed_grad = jnp.dot(latent_grad, down[:, lanes], preferred_element_type=F32)
            piece = jnp.sum(normed_grad * normed, axis=0, keepdims=True)
            for block, pick in enumerate((pick_0, pick_1)):
                row = slice(block, block + 1)
                total = pick * piece
                if not own:
                    total = gain_total[row, lanes] + total
                gain_out[row, lanes] = total
    latent = lax.dot_general(
        scaled[...], down[...], CONTRACT_LAST, preferred_element_type=F32
    ).astype(BF16)
    for start in starts:
        lanes = slice(start, start + STEP_LANES)
        update = jnp.dot(latent, up[:, lanes], preferred_element_type=F32)
        wide = hidden[:, lanes].astype(F32)
        state_out[:, lanes] = jnp.where(active > 0.5, wide + update, wide).astype(BF16)
        grad = lax.dot_general(
            latent, cot[:, lanes], CONTRACT_FIRST, preferred_element_type=F32
        )
        grad_out[:, lanes] = (active * grad).astype(BF16)


HBM = pl.BlockSpec(memory_space=pltpu.HBM)
SMEM = pl.BlockSpec(memory_space=pltpu.SMEM)
VMEM = pl.BlockSpec(memory_space=pltpu.VMEM)


def layer(hidden, embed, cot, gain, gain_total, weights, plan=None):
    own = plan is not None
    rows, width = hidden.shape
    rank = weights[0].shape[2] if own else 2 * weights[0].shape[0]
    if own:
        args = (plan, hidden, embed, cot, gain, *weights)
        specs = (SMEM, HBM, HBM, HBM, VMEM, HBM, HBM)
    else:
        args = (hidden, embed, cot, gain, gain_total, *weights)
        specs = (HBM, HBM, HBM, VMEM, VMEM, HBM, HBM)
    return pl.pallas_call(
        functools.partial(layer_kernel, own),
        out_shape=(
            jax.ShapeDtypeStruct((rows, width), BF16),
            jax.ShapeDtypeStruct((rank, width), BF16),
            jax.ShapeDtypeStruct(gain.shape, F32),
        ),
        in_specs=specs,
        scratch_shapes=[
            pltpu.VMEM((rows, width), BF16),
            pltpu.VMEM((rows, width), BF16),
            pltpu.VMEM((rows, width), BF16),
            pltpu.VMEM((rank, 2 * width), BF16),
            pltpu.VMEM((rank, width), BF16),
            pltpu.VMEM((rank // 2, ID_LANES), BF16),
            pltpu.VMEM((rows, 2 * width), BF16),
            pltpu.SemaphoreType.DMA((8,)),
        ],
        compiler_params=pltpu.CompilerParams(vmem_limit_bytes=66846720),
        name="layer_own" if own else "layer_sent",
    )(*args)


def pack_kernel(slot, plan, down, up, first, second, ids, sems):
    half, width = first.shape[0], up.shape[-1]
    here = slot[0]
    copies = []
    for side, packet in enumerate((first, second)):
        part = pl.ds(side * half, half)
        copies.append((down.at[0, here, part], packet.at[:, pl.ds(0, 2 * width)]))
        copies.append((up.at[0, here, part], packet.at[:, pl.ds(2 * width, width)]))
    block_id = jnp.where(here == 0, plan[0, 0], plan[0, 1])
    ids[...] = jnp.full(ids.shape, block_id, jnp.int32).astype(F32).astype(BF16)
    for packet in (first, second):
        copies.append((ids, packet.at[:, pl.ds(3 * width, ID_LANES)]))
    copies = [pltpu.make_async_copy(a, b, sems.at[i]) for i, (a, b) in enumerate(copies)]
    for copy in copies:
        copy.start()
    for copy in copies:
        copy.wait()


def pack(slot, plan, down, up):
    rank, width = up.shape[2:]
    packet = jax.ShapeDtypeStruct((rank // 2, 3 * width + ID_LANES), BF16)
    return pl.pallas_call(
        pack_kernel,
        out_shape=(packet, packet),
        in_specs=(SMEM, SMEM, HBM, HBM),
        out_specs=(HBM, HBM),
        scratch_shapes=[
            pltpu.VMEM((rank // 2, ID_LANES), BF16),
            pltpu.SemaphoreType.DMA((6,)),
        ],
        name="pack",
    )(slot, plan, down, up)


def exchange(array, axes):
    return lax.all_to_all(array, axes, 0, 0)


def everyone(array, axes, count):
    return exchange(jnp.broadcast_to(array[None], (count,) + array.shape), axes)


def two_parts(wide):
    high = lax.reduce_precision(wide, 8, 7)
    return high, wide - high


def on_device(
    n_z_hi, n_z_lo, n_xh, n_y, n_xl, n_core, hidden_input_rows, embeddings, down, up, gain, plan, cotangent
):
    sections = n_xl * n_core
    position = lax.axis_index("xl") * n_core + lax.axis_index("core")
    hidden, embed, cot = hidden_input_rows[0], embeddings[0], cotangent[0]
    rows, width = hidden.shape
    slots, rank = down.shape[1], down.shape[2]
    ring = ("xh", "xl", "core")

    def weights_route(shift, side):
        route = []
        for xh in range(n_xh):
            for s in range(sections):
                source = (s + shift) % sections
                other = side and source // n_core != s // n_core
                from_xh = (xh + 1) % n_xh if other else xh
                route.append((from_xh * sections + source, xh * sections + s))
        return route

    def section_route(shift):
        return [
            (xh * sections + s, xh * sections + (s + shift) % sections)
            for xh in range(n_xh)
            for s in range(sections)
        ]

    arrived = []
    for shift in range(1, sections):
        slot = (position < shift).astype(jnp.int32).reshape(1)
        packets = pack(slot, plan, down, up)
        sides = []
        for side in range(2):
            sides.append(lax.ppermute(packets[side], ring, weights_route(shift, side)))
        arrived.append(sides)

    state, grad, gain_total = layer(
        hidden, embed, cot, gain, None, (down, up), plan
    )
    wide = grad.astype(F32)
    totals = [wide, jnp.zeros_like(wide)]
    sent = []
    for shift in range(1, sections):
        state, grad, gain_total = layer(
            state, embed, cot, gain, gain_total, arrived[shift - 1]
        )
        sent.append(lax.ppermute(grad, ring, section_route(shift)))
    gain_total = jnp.sum(everyone(gain_total, ("xl", "core"), sections), axis=0)
    final_rows = lax.ppermute(state, ring, section_route(-1))
    for shift, grad in enumerate(sent, 1):
        late = position < shift
        wide = grad.astype(F32)
        totals[0] = totals[0] + jnp.where(late, 0.0, wide)
        totals[1] = totals[1] + jnp.where(late, wide, 0.0)

    near = n_xh * n_y
    deep = slots * rank // near
    gain_lanes = gain.size // (near * deep)
    room = -(-gain_lanes // 128) * 128
    grads = jnp.stack(totals).reshape(near, deep, width)

    def with_gain(grads, gains):
        pad = [(0, 0)] * (gains.ndim - 1) + [(0, room - gains.shape[-1])]
        parts = [jnp.pad(x, pad) for x in two_parts(gains)]
        return jnp.concatenate([grads] + parts, axis=-1).astype(BF16)

    packet = with_gain(grads, gain_total.reshape(near, deep, gain_lanes))
    packet = exchange(packet, ("xh", "y"))
    total = jnp.sum(packet.astype(F32), axis=0)
    for axis, count in (("z_lo", n_z_lo), ("z_hi", n_z_hi)):
        packet = with_gain(
            total[:, :width], total[:, width : width + room] + total[:, width + room :]
        )
        packet = everyone(packet, axis, count)
        total = jnp.sum(packet.astype(F32), axis=0)
    total = with_gain(
        total[:, :width], total[:, width : width + room] + total[:, width + room :]
    )
    total = everyone(total, ("xh", "y"), near)
    total = total.astype(F32)
    scale = 1.0 / math.sqrt(rows * n_xh * n_y * n_z_hi * n_z_lo)
    lora = (total[:, :, :width] * scale).reshape(1, slots, rank, width)
    gains = total[:, :, width : width + gain_lanes]
    gains = gains + total[:, :, width + room : width + room + gain_lanes]
    return final_rows[None], lora, (gains * scale).reshape(gain.shape)


def solution(mesh):
    n_dp, sections = mesh.devices.shape
    n_z_hi, n_z_lo, n_xh, n_xl = 3, 4, 2, 2
    n_y, n_core = n_dp // (n_z_hi * n_z_lo * n_xh), sections // n_xl
    sizes = (n_z_hi, n_z_lo, n_xh, n_y, n_xl, n_core)
    dp, section = ("z_hi", "z_lo", "xh", "y"), ("xl", "core")
    fine = Mesh(np.asarray(mesh.devices).reshape(sizes), dp + section)
    rows = P(section, dp, None)
    weights = P(section, None, None, None)
    return jax.shard_map(
        functools.partial(on_device, *sizes),
        mesh=fine,
        in_specs=(rows, rows, weights, weights, P(), P(section, None), rows),
        out_specs=(rows, weights, P()),
        check_vma=False,
    )
```

time: 195 us -> 311 us (1.59)
  the two profiles are of different devices: /device:TPU:8 before, /device:TPU:1 now
where the time goes in v1:
time: 311 us; the launch traced here: 310 us
  Pallas kernels  158 us (51%)
  blocking collectives  76 us (24%)
  starting transfers between devices  49.2 us (16%)
  waiting for transfers between devices  18.4 us (6%)
  local copies, waits for them, and re-layouts  3.74 us (1%)
  other arithmetic  3.59 us (1%)
    pallas_call x3, Pallas kernels, pack(): pl.pallas_call(pack_kernel, out_shape=(packet, packet), in_specs=(SMEM, S...  131 us
    all_to_all x4, blocking collectives, exchange(): return lax.all_to_all(array, axes, 0, 0)  76 us
    pallas_call x4, Pallas kernels, layer(): pl.pallas_call(functools.partial(layer_kernel, own), out_shape=(jax.Shape...  27.9 us
    ppermute x6, starting transfers between devices, on_device(): sides.append(lax.ppermute(packets[side], ring, weights_route(shift, side)))  26.3 us
    ppermute x1, waiting for transfers between devices, on_device(): final_rows = lax.ppermute(state, ring, section_route(-1))  18.4 us
    ppermute x3, starting transfers between devices, on_device(): sent.append(lax.ppermute(grad, ring, section_route(shift)))  8.08 us
    ppermute x1, starting transfers between devices, on_device(): final_rows = lax.ppermute(state, ring, section_route(-1))  7.72 us
    all_to_all x1, starting transfers between devices, exchange(): return lax.all_to_all(array, axes, 0, 0)  7.03 us
  transfers between devices with their start and end apart: 11, of which 1 were waited for; matrix products, arithmetic and copies ran while one was open for 0% of the time, Pallas kernels for 35%

profile of v1, /device:TPU:1, one launch (start us, length us, event | category | flops | bytes accessed | tf_op | source)
XLA Modules:
  0.0 310.4 jit_solution(3931478272119536357)
XLA Ops:
  0.6 43.5 %pack.3 = (bf16[32,10880]{1,0:T(8,128)(2,1)}, bf16[32,10880]{1,0:T(8,128)(2,1)}) custom-call(s32[1]{0:T(128)} %bitcast.3.slot, s32[1,2]{1,0:T(1,128)} %plan.5, bf16[1,2,64,7168]{3,2,1,0:T(8,128)(2,1)} %down.5, bf16[1,2,64,3584]{3,2,1,0:T(8,128)(2,1)} %up.5), custom_call_target="tpu_custom_call" | custom-call | tf_op jit(solution)/shard_map/pack/pallas_call | solution.py:166
  44.2 12.4 %collective-permute-start = (bf16[32,10880]{1,0:T(8,128)(2,1)}, bf16[32,10880]{1,0:T(8,128)(2,1)}, u32[]{:S(2)}, u32[]{:S(2)}) collective-permute-start(bf16[32,10880]{1,0:T(8,128)(2,1)} %get-tuple-element.23), channel_id=1, source_target_pairs={{1,0},{2,1},{3,2},{0,3},{33,32},{34,33},{35,34},{32,35},{5,4},{6,5... | collective-permute-start | bytes 2088968 | tf_op jit(solution)/shard_map/ppermute | solution.py:225
  56.6 1.9 collective-permute-start.1
  58.5 43.5 %pack.4 = (bf16[32,10880]{1,0:T(8,128)(2,1)}, bf16[32,10880]{1,0:T(8,128)(2,1)}) custom-call(s32[1]{0:T(128)} %bitcast.4.slot, s32[1,2]{1,0:T(1,128)} %plan.5, bf16[1,2,64,7168]{3,2,1,0:T(8,128)(2,1)} %down.5, bf16[1,2,64,3584]{3,2,1,0:T(8,128)(2,1)} %up.5), custom_call_target="tpu_custom_call" | custom-call | tf_op jit(solution)/shard_map/pack/pallas_call | solution.py:166
  102.0 1.9 collective-permute-start.2
  104.0 1.9 collective-permute-start.3
  105.9 43.5 %pack.5 = (bf16[32,10880]{1,0:T(8,128)(2,1)}, bf16[32,10880]{1,0:T(8,128)(2,1)}) custom-call(s32[1]{0:T(128)} %bitcast.5.slot, s32[1,2]{1,0:T(1,128)} %plan.5, bf16[1,2,64,7168]{3,2,1,0:T(8,128)(2,1)} %down.5, bf16[1,2,64,3584]{3,2,1,0:T(8,128)(2,1)} %up.5), custom_call_target="tpu_custom_call" | custom-call | tf_op jit(solution)/shard_map/pack/pallas_call | solution.py:166
  149.4 6.3 %collective-permute-start.4 = (bf16[32,10880]{1,0:T(8,128)(2,1)}, bf16[32,10880]{1,0:T(8,128)(2,1)}, u32[]{:S(2)}, u32[]{:S(2)}) collective-permute-start(bf16[32,10880]{1,0:T(8,128)(2,1)} %get-tuple-element.31), channel_id=1, source_target_pairs={{3,0},{0,1},{1,2},{2,3},{35,32},{32,33},{33,34},{34,35},{7,4},{4,5... | collective-permute-start | bytes 2088968 | tf_op jit(solution)/shard_map/ppermute | solution.py:225
  155.7 0.0 collective-permute-done.refs_5_
  155.7 1.9 collective-permute-start.5
  157.6 7.0 %layer_own.1 = (bf16[128,3584]{1,0:T(8,128)(2,1)}, bf16[64,3584]{1,0:T(8,128)(2,1)}, f32[2,7168]{1,0:T(2,128)}) custom-call(s32[1,2]{1,0:T(1,128)} %plan.5, bf16[128,3584]{1,0:T(8,128)(2,1)} %bitcast.24, bf16[128,3584]{1,0:T(8,128)(2,1)} %bitcast.13, bf16[128,3584]{1,0:T(8,128)(2,1)} %bitcast.17, f32[2,7168]{1,0:T(2,128)} %refs_3_.5, ...), custom_call_target="tpu_custom_call" | custom-call | tf_op jit(solution)/shard_map/layer_own/pallas_call | solution.py:121
  164.6 0.0 collective-permute-done.1.refs_6_
  164.6 7.0 %layer_sent.3 = (bf16[128,3584]{1,0:T(8,128)(2,1)}, bf16[64,3584]{1,0:T(8,128)(2,1)}, f32[2,7168]{1,0:T(2,128)}) custom-call(bf16[128,3584]{1,0:T(8,128)(2,1)} %get-tuple-element.21.refs_0_, bf16[128,3584]{1,0:T(8,128)(2,1)} %bitcast.14, bf16[128,3584]{1,0:T(8,128)(2,1)} %bitcast.18, f32[2,7168]{1,0:T(2,128)} %refs_3_.5, ...), custom_call_target="tpu_custom_call" | custom-call | tf_op jit(solution)/shard_map/layer_sent/pallas_call | solution.py:121
  171.6 0.0 collective-permute-done.2.refs_5_
  171.6 0.0 collective-permute-done.3.refs_6_
  171.6 7.0 %layer_sent.4 = (bf16[128,3584]{1,0:T(8,128)(2,1)}, bf16[64,3584]{1,0:T(8,128)(2,1)}, f32[2,7168]{1,0:T(2,128)}) custom-call(bf16[128,3584]{1,0:T(8,128)(2,1)} %get-tuple-element.25.refs_0_, bf16[128,3584]{1,0:T(8,128)(2,1)} %bitcast.15, bf16[128,3584]{1,0:T(8,128)(2,1)} %bitcast.19, f32[2,7168]{1,0:T(2,128)} %refs_3_.5, ...), custom_call_target="tpu_custom_call" | custom-call | tf_op jit(solution)/shard_map/layer_sent/pallas_call | solution.py:121
  178.6 0.0 collective-permute-done.4.refs_5_
  178.6 0.0 collective-permute-done.5.refs_6_
  178.6 7.0 %layer_sent.5 = (bf16[128,3584]{1,0:T(8,128)(2,1)}, bf16[64,3584]{1,0:T(8,128)(2,1)}, f32[2,7168]{1,0:T(2,128)}) custom-call(bf16[128,3584]{1,0:T(8,128)(2,1)} %get-tuple-element.29.refs_0_, bf16[128,3584]{1,0:T(8,128)(2,1)} %bitcast.16, bf16[128,3584]{1,0:T(8,128)(2,1)} %bitcast.20, f32[2,7168]{1,0:T(2,128)} %refs_3_.5, ...), custom_call_target="tpu_custom_call" | custom-call | tf_op jit(solution)/shard_map/layer_sent/pallas_call | solution.py:121
  185.6 2.4 collective-permute-start.9
  188.0 2.2 collective-permute-start.8
  190.3 3.4 %collective-permute-start.7 = (bf16[64,3584]{1,0:T(8,128)(2,1)}, bf16[64,3584]{1,0:T(8,128)(2,1)S(1)}, u32[]{:S(2)}, u32[]{:S(2)}) collective-permute-start(bf16[64,3584]{1,0:T(8,128)(2,1)} %get-tuple-element.35), channel_id=1, source_target_pairs={{0,1},{1,2},{2,3},{3,0},{32,33},{33,34},{34,35},{35,32},{4,5},{5,6... | collective-permute-start | bytes 1376264 | tf_op jit(solution)/shard_map/ppermute | solution.py:238
  193.7 0.9 broadcast_in_dim.39
  194.6 18.3 %all_to_all.25 = f32[4,2,7168]{2,1,0:T(2,128)S(1)} all-to-all(f32[4,2,7168]{2,1,0:T(2,128)S(1)} %broadcast_in_dim.39), channel_id=1, replica_groups=mesh['z_hi'=3,'z_lo'=4,'xh'=2,'y'=8,'xl'=2,'core'=2] {'xl','core'}, dimensions={0} | all-to-all | bytes 458752 | tf_op jit(solution)/shard_map/all_to_all | solution.py:180
  212.8 0.1 reduce_sum.36
  212.9 0.1 reshape.108
  213.1 0.0 collective-permute-done.9
  213.1 0.0 collective-permute-done.8
  213.1 0.0 collective-permute-done.7
  213.1 1.5 fusion.13
  214.6 0.1 pad_maximum_fusion
  214.7 0.1 fusion.4
  214.8 27.8 %all_to_all.26 = bf16[16,8,3840]{2,1,0:T(8,128)(2,1)S(1)} all-to-all(bf16[16,8,3840]{2,1,0:T(8,128)(2,1)S(1)} %fusion.4), channel_id=1, replica_groups=mesh['z_hi'=3,'z_lo'=4,'xh'=2,'y'=8,'xl'=2,'core'=2] {'xh','y'}, dimensions={0} | all-to-all | bytes 1966080 | tf_op jit(solution)/shard_map/all_to_all | solution.py:180
  242.6 0.1 convert_reduce_fusion
  242.8 9.8 %all_to_all.27 = bf16[4,8,3840]{2,1,0:T(8,128)(2,1)S(1)} all-to-all(bf16[4,8,3840]{2,1,0:T(8,128)(2,1)S(1)} %broadcast_in_dim.40), channel_id=1, replica_groups=mesh['z_hi'=3,'z_lo'=4,'xh'=2,'y'=8,'xl'=2,'core'=2] {'z_lo'}, dimensions={0} | all-to-all | bytes 491520 | tf_op jit(solution)/shard_map/all_to_all | solution.py:180
  252.8 0.0 copy-start
  252.8 20.0 %all_to_all.28 = bf16[3,8,3840]{2,1,0:T(8,128)(2,1)S(1)} all-to-all(bf16[3,8,3840]{2,1,0:T(8,128)(2,1)S(1)} %broadcast_in_dim.41), channel_id=1, replica_groups=mesh['z_hi'=3,'z_lo'=4,'xh'=2,'y'=8,'xl'=2,'core'=2] {'z_hi'}, dimensions={0} | all-to-all | bytes 368640 | tf_op jit(solution)/shard_map/all_to_all | solution.py:180
  272.9 1.0 broadcast_in_dim.42
  273.9 7.0 %all-to-all-start.4 = ((bf16[16,8,3840]{2,1,0:T(8,128)(2,1)}), bf16[16,8,3840]{2,1,0:T(8,128)(2,1)S(1)}, u32[]{:S(2)}, u32[]{:S(2)}) async-start(bf16[16,8,3840]{2,1,0:T(8,128)(2,1)} %broadcast_in_dim.42), calls=%async_computation.4 | async-start | bytes 1966080 | tf_op jit(solution)/shard_map/all_to_all | solution.py:180
  280.9 0.0 copy-done
  280.9 7.7 %collective-permute-start.6 = (bf16[128,3584]{1,0:T(8,128)(2,1)S(1)}, bf16[128,3584]{1,0:T(8,128)(2,1)S(1)}, u32[]{:S(2)}, u32[]{:S(2)}) collective-permute-start(bf16[128,3584]{1,0:T(8,128)(2,1)S(1)} %copy-done), channel_id=1, source_target_pairs={{0,3},{1,0},{2,1},{3,2},{32,35},{33,32},{34,33},{35,34},{4,7},{5,4... | collective-permute-start | bytes 2752520 | tf_op jit(solution)/shard_map/ppermute | solution.py:240
  288.7 18.4 %collective-permute-done.6 = bf16[128,3584]{1,0:T(8,128)(2,1)S(1)} collective-permute-done((bf16[128,3584]{1,0:T(8,128)(2,1)S(1)}, bf16[128,3584]{1,0:T(8,128)(2,1)S(1)}, u32[]{:S(2)}, u32[]{:S(2)}) %collective-permute-start.6) | collective-permute-done | bytes 917536 | tf_op jit(solution)/shard_map/ppermute | solution.py:240
  307.1 0.0 all-to-all-done.4
  307.1 0.1 convert_element_type.53
  307.2 1.5 slice_multiply_fusion
  308.7 0.8 reshape.110
  309.4 0.9 copy.13
  (15 shorter events, 0.2 us)
Async XLA Ops:
  44.2 111.5 %collective-permute-start = (bf16[32,10880]{1,0:T(8,128)(2,1)}, bf16[32,10880]{1,0:T(8,128)(2,1)}, u32[]{:S(2)}, u32[]{:S(2)}) collective-permute-start(bf16[32,10880]{1,0:T(8,128)(2,1)} %get-tuple-element.23), channel_id=1, source_target_pairs={{1,0},{2,1},{3,2},{0,3},{33,32},{34,33},{35,34},{32,35},{5,4},{6,5... | collective-permute-start | bytes 2088968 | tf_op jit(solution)/shard_map/ppermute | solution.py:225
  56.6 108.0 %collective-permute-start.1 = (bf16[32,10880]{1,0:T(8,128)(2,1)}, bf16[32,10880]{1,0:T(8,128)(2,1)}, u32[]{:S(2)}, u32[]{:S(2)}) collective-permute-start(bf16[32,10880]{1,0:T(8,128)(2,1)} %get-tuple-element.24), channel_id=1, source_target_pairs={{1,0},{34,1},{3,2},{32,3},{33,32},{2,33},{35,34},{0,35},{5,4},{38,... | collective-permute-start | bytes 2088968 | tf_op jit(solution)/shard_map/ppermute | solution.py:225
  102.0 69.5 %collective-permute-start.2 = (bf16[32,10880]{1,0:T(8,128)(2,1)}, bf16[32,10880]{1,0:T(8,128)(2,1)}, u32[]{:S(2)}, u32[]{:S(2)}) collective-permute-start(bf16[32,10880]{1,0:T(8,128)(2,1)} %get-tuple-element.27), channel_id=1, source_target_pairs={{2,0},{3,1},{0,2},{1,3},{34,32},{35,33},{32,34},{33,35},{6,4},{7,5... | collective-permute-start | bytes 2088968 | tf_op jit(solution)/shard_map/ppermute | solution.py:225
  104.0 67.6 %collective-permute-start.3 = (bf16[32,10880]{1,0:T(8,128)(2,1)}, bf16[32,10880]{1,0:T(8,128)(2,1)}, u32[]{:S(2)}, u32[]{:S(2)}) collective-permute-start(bf16[32,10880]{1,0:T(8,128)(2,1)} %get-tuple-element.28), channel_id=1, source_target_pairs={{34,0},{35,1},{32,2},{33,3},{2,32},{3,33},{0,34},{1,35},{38,4},{39... | collective-permute-start | bytes 2088968 | tf_op jit(solution)/shard_map/ppermute | solution.py:225
  149.4 29.2 %collective-permute-start.4 = (bf16[32,10880]{1,0:T(8,128)(2,1)}, bf16[32,10880]{1,0:T(8,128)(2,1)}, u32[]{:S(2)}, u32[]{:S(2)}) collective-permute-start(bf16[32,10880]{1,0:T(8,128)(2,1)} %get-tuple-element.31), channel_id=1, source_target_pairs={{3,0},{0,1},{1,2},{2,3},{35,32},{32,33},{33,34},{34,35},{7,4},{4,5... | collective-permute-start | bytes 2088968 | tf_op jit(solution)/shard_map/ppermute | solution.py:225
  155.7 22.9 %collective-permute-start.5 = (bf16[32,10880]{1,0:T(8,128)(2,1)}, bf16[32,10880]{1,0:T(8,128)(2,1)}, u32[]{:S(2)}, u32[]{:S(2)}) collective-permute-start(bf16[32,10880]{1,0:T(8,128)(2,1)} %get-tuple-element.32), channel_id=1, source_target_pairs={{35,0},{0,1},{33,2},{2,3},{3,32},{32,33},{1,34},{34,35},{39,4},{4,... | collective-permute-start | bytes 2088968 | tf_op jit(solution)/shard_map/ppermute | solution.py:225
  185.6 27.5 %collective-permute-start.9 = (bf16[64,3584]{1,0:T(8,128)(2,1)}, bf16[64,3584]{1,0:T(8,128)(2,1)S(1)}, u32[]{:S(2)}, u32[]{:S(2)}) collective-permute-start(bf16[64,3584]{1,0:T(8,128)(2,1)} %get-tuple-element.37), channel_id=1, source_target_pairs={{0,3},{1,0},{2,1},{3,2},{32,35},{33,32},{34,33},{35,34},{4,7},{5,4... | collective-permute-start | bytes 1376264 | tf_op jit(solution)/shard_map/ppermute | solution.py:238
  188.0 25.1 %collective-permute-start.8 = (bf16[64,3584]{1,0:T(8,128)(2,1)}, bf16[64,3584]{1,0:T(8,128)(2,1)S(1)}, u32[]{:S(2)}, u32[]{:S(2)}) collective-permute-start(bf16[64,3584]{1,0:T(8,128)(2,1)} %get-tuple-element.36), channel_id=1, source_target_pairs={{0,2},{1,3},{2,0},{3,1},{32,34},{33,35},{34,32},{35,33},{4,6},{5,7... | collective-permute-start | bytes 1376264 | tf_op jit(solution)/shard_map/ppermute | solution.py:238
  190.3 22.8 %collective-permute-start.7 = (bf16[64,3584]{1,0:T(8,128)(2,1)}, bf16[64,3584]{1,0:T(8,128)(2,1)S(1)}, u32[]{:S(2)}, u32[]{:S(2)}) collective-permute-start(bf16[64,3584]{1,0:T(8,128)(2,1)} %get-tuple-element.35), channel_id=1, source_target_pairs={{0,1},{1,2},{2,3},{3,0},{32,33},{33,34},{34,35},{35,32},{4,5},{5,6... | collective-permute-start | bytes 1376264 | tf_op jit(solution)/shard_map/ppermute | solution.py:238
  252.8 28.2 %copy-start = (bf16[128,3584]{1,0:T(8,128)(2,1)S(1)}, bf16[128,3584]{1,0:T(8,128)(2,1)}, u32[]{:S(2)}) copy-start(bf16[128,3584]{1,0:T(8,128)(2,1)} %get-tuple-element.33) | copy-start | bytes 2752516
  273.9 33.2 %all-to-all-start.4 = ((bf16[16,8,3840]{2,1,0:T(8,128)(2,1)}), bf16[16,8,3840]{2,1,0:T(8,128)(2,1)S(1)}, u32[]{:S(2)}, u32[]{:S(2)}) async-start(bf16[16,8,3840]{2,1,0:T(8,128)(2,1)} %broadcast_in_dim.42), calls=%async_computation.4 | async-start | bytes 1966080 | tf_op jit(solution)/shard_map/all_to_all | solution.py:180
  280.9 26.1 %collective-permute-start.6 = (bf16[128,3584]{1,0:T(8,128)(2,1)S(1)}, bf16[128,3584]{1,0:T(8,128)(2,1)S(1)}, u32[]{:S(2)}, u32[]{:S(2)}) collective-permute-start(bf16[128,3584]{1,0:T(8,128)(2,1)S(1)} %copy-done), channel_id=1, source_target_pairs={{0,3},{1,0},{2,1},{3,2},{32,35},{33,32},{34,33},{35,34},{4,7},{5,4... | collective-permute-start | bytes 2752520 | tf_op jit(solution)/shard_map/ppermute | solution.py:240

commit v2 on v1

--- a/solution.py
+++ b/solution.py
@@ -16,18 +16,17 @@
 STEP_LANES = 512
 ID_LANES = 128
 CONTRACT_LAST = (((1,), (1,)), ((), ()))
-CONTRACT_FIRST = (((0,), (0,)), ((), ()))
 
 
 def layer_kernel(own, *refs):
     if own:
         plan, hidden_in, embed_in, cot_in, gain, down_in, up_in = refs[:7]
-        rest = refs[7:]
+        state_out, grad_out, gain_out, squares_ref, *rest = refs[7:]
         gain_total = None
     else:
-        hidden_in, embed_in, cot_in, gain, gain_total, first, second = refs[:7]
-        rest = refs[7:]
-    state_out, grad_out, gain_out, hidden, embed, cot, down, up, ids, scaled, sems = rest
+        hidden_in, embed_in, cot_in, gain, gain_total, squares_ref, first, second = refs[:8]
+        state_out, grad_out, gain_out, *rest = refs[8:]
+    hidden, embed, cot, down, up, ids, scaled, sems = rest
     rows, width = hidden.shape
     half = down.shape[0] // 2
     moves = [(hidden_in, hidden), (embed_in, embed), (cot_in, cot)]
@@ -49,14 +48,22 @@
         copy.start()
 
     starts = range(0, width, STEP_LANES)
-    squares = jnp.zeros((rows, ID_LANES), F32)
-    for copy, source in zip(copies[:2], (hidden, embed)):
-        copy.wait()
+
+    def squares_of(source):
+        squares = jnp.zeros((rows, ID_LANES), F32)
         for start in starts:
             wide = source[:, start : start + STEP_LANES].astype(F32)
             wide = wide * wide
             for lane in range(0, STEP_LANES, ID_LANES):
                 squares = squares + wide[:, lane : lane + ID_LANES]
+        return squares
+
+    copies[0].wait()
+    squares = squares_of(hidden)
+    copies[1].wait()
+    if own:
+        squares_ref[...] = squares_of(embed)
+    squares = squares + squares_ref[...]
     squares_sum = jnp.sum(squares, axis=1, keepdims=True)
     inverse = lax.rsqrt(squares_sum / (2 * width) + 1e-05)
 
@@ -92,14 +99,13 @@
     latent = lax.dot_general(
         scaled[...], down[...], CONTRACT_LAST, preferred_element_type=F32
     ).astype(BF16)
+    latent_turned = latent.astype(F32).T.astype(BF16)
     for start in starts:
         lanes = slice(start, start + STEP_LANES)
         update = jnp.dot(latent, up[:, lanes], preferred_element_type=F32)
         wide = hidden[:, lanes].astype(F32)
         state_out[:, lanes] = jnp.where(active > 0.5, wide + update, wide).astype(BF16)
-        grad = lax.dot_general(
-            latent, cot[:, lanes], CONTRACT_FIRST, preferred_element_type=F32
-        )
+        grad = jnp.dot(latent_turned, cot[:, lanes], preferred_element_type=F32)
         grad_out[:, lanes] = (active * grad).astype(BF16)
 
 
@@ -108,7 +114,7 @@
 VMEM = pl.BlockSpec(memory_space=pltpu.VMEM)
 
 
-def layer(hidden, embed, cot, gain, gain_total, weights, plan=None):
+def layer(hidden, embed, cot, gain, carried, weights, plan=None):
     own = plan is not None
     rows, width = hidden.shape
     rank = weights[0].shape[2] if own else 2 * weights[0].shape[0]
@@ -116,15 +122,16 @@
         args = (plan, hidden, embed, cot, gain, *weights)
         specs = (SMEM, HBM, HBM, HBM, VMEM, HBM, HBM)
     else:
-        args = (hidden, embed, cot, gain, gain_total, *weights)
-        specs = (HBM, HBM, HBM, VMEM, VMEM, HBM, HBM)
+        args = (hidden, embed, cot, gain, *carried, *weights)
+        specs = (HBM, HBM, HBM, VMEM, VMEM, VMEM, HBM, HBM)
     return pl.pallas_call(
         functools.partial(layer_kernel, own),
         out_shape=(
             jax.ShapeDtypeStruct((rows, width), BF16),
             jax.ShapeDtypeStruct((rank, width), BF16),
             jax.ShapeDtypeStruct(gain.shape, F32),
-        ),
+        )
+        + ((jax.ShapeDtypeStruct((rows, ID_LANES), F32),) if own else ()),
         in_specs=specs,
         scratch_shapes=[
             pltpu.VMEM((rows, width), BF16),
@@ -141,39 +148,36 @@
     )(*args)
 
 
-def pack_kernel(slot, plan, down, up, first, second, ids, sems):
-    half, width = first.shape[0], up.shape[-1]
-    here = slot[0]
-    copies = []
-    for side, packet in enumerate((first, second)):
-        part = pl.ds(side * half, half)
-        copies.append((down.at[0, here, part], packet.at[:, pl.ds(0, 2 * width)]))
-        copies.append((up.at[0, here, part], packet.at[:, pl.ds(2 * width, width)]))
-    block_id = jnp.where(here == 0, plan[0, 0], plan[0, 1])
-    ids[...] = jnp.full(ids.shape, block_id, jnp.int32).astype(F32).astype(BF16)
-    for packet in (first, second):
-        copies.append((ids, packet.at[:, pl.ds(3 * width, ID_LANES)]))
-    copies = [pltpu.make_async_copy(a, b, sems.at[i]) for i, (a, b) in enumerate(copies)]
-    for copy in copies:
-        copy.start()
-    for copy in copies:
-        copy.wait()
+def pack_kernel(slot, down, up, plan, *packets):
+    width, half = up.shape[-1], packets[0].shape[0]
+    block_id = jnp.where(slot[0] == 0, plan[0, 0], plan[0, 1])
+    for side, packet in enumerate(packets):
+        rows = slice(side * half, (side + 1) * half)
+        packet[:, : 2 * width] = down[0, 0, rows, :]
+        packet[:, 2 * width : 3 * width] = up[0, 0, rows, :]
+        ids = jnp.full((half, ID_LANES), block_id, jnp.int32)
+        packet[:, 3 * width :] = ids.astype(F32).astype(BF16)
 
 
 def pack(slot, plan, down, up):
     rank, width = up.shape[2:]
     packet = jax.ShapeDtypeStruct((rank // 2, 3 * width + ID_LANES), BF16)
+    whole = pl.BlockSpec(packet.shape, lambda i, slot: (0, 0))
     return pl.pallas_call(
         pack_kernel,
         out_shape=(packet, packet),
-        in_specs=(SMEM, SMEM, HBM, HBM),
-        out_specs=(HBM, HBM),
-        scratch_shapes=[
-            pltpu.VMEM((rank // 2, ID_LANES), BF16),
-            pltpu.SemaphoreType.DMA((6,)),
-        ],
+        grid_spec=pltpu.PrefetchScalarGridSpec(
+            num_scalar_prefetch=1,
+            grid=(1,),
+            in_specs=[
+                pl.BlockSpec((1, 1, rank, 2 * width), lambda i, slot: (0, slot[0], 0, 0)),
+                pl.BlockSpec((1, 1, rank, width), lambda i, slot: (0, slot[0], 0, 0)),
+                SMEM,
+            ],
+            out_specs=(whole, whole),
+        ),
         name="pack",
-    )(slot, plan, down, up)
+    )(slot, down, up, plan)
 
 
 def exchange(array, axes):
@@ -225,15 +229,15 @@
             sides.append(lax.ppermute(packets[side], ring, weights_route(shift, side)))
         arrived.append(sides)
 
-    state, grad, gain_total = layer(
-        hidden, embed, cot, gain, None, (down, up), plan
+    state, grad, gain_total, squares = layer(
+        hidden, embed, cot, gain, (), (down, up), plan
     )
     wide = grad.astype(F32)
     totals = [wide, jnp.zeros_like(wide)]
     sent = []
     for shift in range(1, sections):
         state, grad, gain_total = layer(
-            state, embed, cot, gain, gain_total, arrived[shift - 1]
+            state, embed, cot, gain, (gain_total, squares), arrived[shift - 1]
         )
         sent.append(lax.ppermute(grad, ring, section_route(shift)))
     gain_total = jnp.sum(everyone(gain_total, ("xl", "core"), sections), axis=0)

time: 311 us -> 188 us (0.60)
  Pallas kernels: 158 us -> 35.4 us
    pallas_call x3, Pallas kernels: 131 us -> 7.31 us  [pack(): pl.pallas_call(pack_kernel, out_shape=(packet, packet), grid_spec=pltpu.P...]
  transfers between devices with their start and end apart: 11 -> 11, of which waited for: 1 -> 1; matrix products, arithmetic and copies ran while one was open for 0% -> 1% of each run, Pallas kernels for 35% -> 14%
where the time goes in v2:
time: 188 us; the launch traced here: 187 us
  blocking collectives  75.8 us (40%)
  starting transfers between devices  49.3 us (26%)
  Pallas kernels  35.4 us (19%)
  waiting for transfers between devices  18.4 us (10%)
  local copies, waits for them, and re-layouts  3.74 us (2%)
  other arithmetic  3.59 us (2%)
    all_to_all x4, blocking collectives, exchange(): return lax.all_to_all(array, axes, 0, 0)  75.8 us
    pallas_call x4, Pallas kernels, layer(): pl.pallas_call(functools.partial(layer_kernel, own), out_shape=(jax.Shape...  28.1 us
    ppermute x6, starting transfers between devices, on_device(): sides.append(lax.ppermute(packets[side], ring, weights_route(shift, side)))  26.3 us
    ppermute x1, waiting for transfers between devices, on_device(): final_rows = lax.ppermute(state, ring, section_route(-1))  18.4 us
    ppermute x3, starting transfers between devices, on_device(): sent.append(lax.ppermute(grad, ring, section_route(shift)))  8.27 us
    ppermute x1, starting transfers between devices, on_device(): final_rows = lax.ppermute(state, ring, section_route(-1))  7.72 us
    pallas_call x3, Pallas kernels, pack(): pl.pallas_call(pack_kernel, out_shape=(packet, packet), grid_spec=pltpu.P...  7.31 us
    all_to_all x1, starting transfers between devices, exchange(): return lax.all_to_all(array, axes, 0, 0)  7.03 us
  transfers between devices with their start and end apart: 11, of which 1 were waited for; matrix products, arithmetic and copies ran while one was open for 1% of the time, Pallas kernels for 14%

profile of v2, /device:TPU:1, one launch (start us, length us, event | category | flops | bytes accessed | tf_op | source)
XLA Modules:
  0.0 187.2 jit_solution(1477047712933979263)
XLA Ops:
  0.6 2.4 %pack.3 = (bf16[32,10880]{1,0:T(8,128)(2,1)}, bf16[32,10880]{1,0:T(8,128)(2,1)}) custom-call(s32[1]{0:T(128)} %bitcast.3.slot, bf16[1,2,64,7168]{3,2,1,0:T(8,128)(2,1)} %down.5, bf16[1,2,64,3584]{3,2,1,0:T(8,128)(2,1)} %up.5, s32[1,2]{1,0:T(1,128)} %plan.5), custom_call_target="tpu_custom_call" | custom-call | tf_op jit(solution)/shard_map/pack/pallas_call | solution.py:166
  3.1 12.4 %collective-permute-start = (bf16[32,10880]{1,0:T(8,128)(2,1)}, bf16[32,10880]{1,0:T(8,128)(2,1)}, u32[]{:S(2)}, u32[]{:S(2)}) collective-permute-start(bf16[32,10880]{1,0:T(8,128)(2,1)} %get-tuple-element.25), channel_id=1, source_target_pairs={{1,0},{2,1},{3,2},{0,3},{33,32},{34,33},{35,34},{32,35},{5,4},{6,5... | collective-permute-start | bytes 2088968 | tf_op jit(solution)/shard_map/ppermute | solution.py:229
  15.5 1.9 %collective-permute-start.1 = (bf16[32,10880]{1,0:T(8,128)(2,1)}, bf16[32,10880]{1,0:T(8,128)(2,1)}, u32[]{:S(2)}, u32[]{:S(2)}) collective-permute-start(bf16[32,10880]{1,0:T(8,128)(2,1)} %get-tuple-element.26), channel_id=1, source_target_pairs={{1,0},{34,1},{3,2},{32,3},{33,32},{2,33},{35,34},{0,35},{5,4},{38,... | collective-permute-start | bytes 2088968 | tf_op jit(solution)/shard_map/ppermute | solution.py:229
  17.4 2.4 %pack.4 = (bf16[32,10880]{1,0:T(8,128)(2,1)}, bf16[32,10880]{1,0:T(8,128)(2,1)}) custom-call(s32[1]{0:T(128)} %bitcast.4.slot, bf16[1,2,64,7168]{3,2,1,0:T(8,128)(2,1)} %down.5, bf16[1,2,64,3584]{3,2,1,0:T(8,128)(2,1)} %up.5, s32[1,2]{1,0:T(1,128)} %plan.5), custom_call_target="tpu_custom_call" | custom-call | tf_op jit(solution)/shard_map/pack/pallas_call | solution.py:166
  19.8 1.9 %collective-permute-start.2 = (bf16[32,10880]{1,0:T(8,128)(2,1)}, bf16[32,10880]{1,0:T(8,128)(2,1)}, u32[]{:S(2)}, u32[]{:S(2)}) collective-permute-start(bf16[32,10880]{1,0:T(8,128)(2,1)} %get-tuple-element.29), channel_id=1, source_target_pairs={{2,0},{3,1},{0,2},{1,3},{34,32},{35,33},{32,34},{33,35},{6,4},{7,5... | collective-permute-start | bytes 2088968 | tf_op jit(solution)/shard_map/ppermute | solution.py:229
  21.7 1.9 %collective-permute-start.3 = (bf16[32,10880]{1,0:T(8,128)(2,1)}, bf16[32,10880]{1,0:T(8,128)(2,1)}, u32[]{:S(2)}, u32[]{:S(2)}) collective-permute-start(bf16[32,10880]{1,0:T(8,128)(2,1)} %get-tuple-element.30), channel_id=1, source_target_pairs={{34,0},{35,1},{32,2},{33,3},{2,32},{3,33},{0,34},{1,35},{38,4},{39... | collective-permute-start | bytes 2088968 | tf_op jit(solution)/shard_map/ppermute | solution.py:229
  23.7 2.4 %pack.5 = (bf16[32,10880]{1,0:T(8,128)(2,1)}, bf16[32,10880]{1,0:T(8,128)(2,1)}) custom-call(s32[1]{0:T(128)} %bitcast.5.slot, bf16[1,2,64,7168]{3,2,1,0:T(8,128)(2,1)} %down.5, bf16[1,2,64,3584]{3,2,1,0:T(8,128)(2,1)} %up.5, s32[1,2]{1,0:T(1,128)} %plan.5), custom_call_target="tpu_custom_call" | custom-call | tf_op jit(solution)/shard_map/pack/pallas_call | solution.py:166
  26.1 6.2 %collective-permute-start.4 = (bf16[32,10880]{1,0:T(8,128)(2,1)}, bf16[32,10880]{1,0:T(8,128)(2,1)}, u32[]{:S(2)}, u32[]{:S(2)}) collective-permute-start(bf16[32,10880]{1,0:T(8,128)(2,1)} %get-tuple-element.33), channel_id=1, source_target_pairs={{3,0},{0,1},{1,2},{2,3},{35,32},{32,33},{33,34},{34,35},{7,4},{4,5... | collective-permute-start | bytes 2088968 | tf_op jit(solution)/shard_map/ppermute | solution.py:229
  32.4 0.0 collective-permute-done.refs_6_
  32.4 1.9 %collective-permute-start.5 = (bf16[32,10880]{1,0:T(8,128)(2,1)}, bf16[32,10880]{1,0:T(8,128)(2,1)}, u32[]{:S(2)}, u32[]{:S(2)}) collective-permute-start(bf16[32,10880]{1,0:T(8,128)(2,1)} %get-tuple-element.34), channel_id=1, source_target_pairs={{35,0},{0,1},{33,2},{2,3},{3,32},{32,33},{1,34},{34,35},{39,4},{4,... | collective-permute-start | bytes 2088968 | tf_op jit(solution)/shard_map/ppermute | solution.py:229
  34.3 7.0 %layer_own.1 = (bf16[128,3584]{1,0:T(8,128)(2,1)}, bf16[64,3584]{1,0:T(8,128)(2,1)}, f32[2,7168]{1,0:T(2,128)}, f32[128,128]{1,0:T(8,128)}) custom-call(s32[1,2]{1,0:T(1,128)} %plan.5, bf16[128,3584]{1,0:T(8,128)(2,1)} %bitcast.24, bf16[128,3584]{1,0:T(8,128)(2,1)} %bitcast.13, bf16[128,3584]{1,0:T(8,128)(2,1)} %bitcast.17, f32[2,7168]{1,0:T(2,128)} %refs_3_.5, ...), custom_call_target="tpu_custom_call" | custom-call | tf_op jit(solution)/shard_map/layer_own/pallas_call | solution.py:127
  41.3 0.0 collective-permute-done.1.refs_7_
  41.3 7.0 %layer_sent.3 = (bf16[128,3584]{1,0:T(8,128)(2,1)}, bf16[64,3584]{1,0:T(8,128)(2,1)}, f32[2,7168]{1,0:T(2,128)}) custom-call(bf16[128,3584]{1,0:T(8,128)(2,1)} %get-tuple-element.22.refs_0_, bf16[128,3584]{1,0:T(8,128)(2,1)} %bitcast.14, bf16[128,3584]{1,0:T(8,128)(2,1)} %bitcast.18, f32[2,7168]{1,0:T(2,128)} %refs_3_.5, ...), custom_call_target="tpu_custom_call" | custom-call | tf_op jit(solution)/shard_map/layer_sent/pallas_call | solution.py:127
  48.3 0.0 collective-permute-done.2.refs_6_
  48.3 0.0 collective-permute-done.3.refs_7_
  48.3 7.1 %layer_sent.4 = (bf16[128,3584]{1,0:T(8,128)(2,1)}, bf16[64,3584]{1,0:T(8,128)(2,1)}, f32[2,7168]{1,0:T(2,128)}) custom-call(bf16[128,3584]{1,0:T(8,128)(2,1)} %get-tuple-element.27.refs_0_, bf16[128,3584]{1,0:T(8,128)(2,1)} %bitcast.15, bf16[128,3584]{1,0:T(8,128)(2,1)} %bitcast.19, f32[2,7168]{1,0:T(2,128)} %refs_3_.5, ...), custom_call_target="tpu_custom_call" | custom-call | tf_op jit(solution)/shard_map/layer_sent/pallas_call | solution.py:127
  55.4 0.0 collective-permute-done.4.refs_6_
  55.4 0.0 collective-permute-done.5.refs_7_
  55.4 7.0 %layer_sent.5 = (bf16[128,3584]{1,0:T(8,128)(2,1)}, bf16[64,3584]{1,0:T(8,128)(2,1)}, f32[2,7168]{1,0:T(2,128)}) custom-call(bf16[128,3584]{1,0:T(8,128)(2,1)} %get-tuple-element.31.refs_0_, bf16[128,3584]{1,0:T(8,128)(2,1)} %bitcast.16, bf16[128,3584]{1,0:T(8,128)(2,1)} %bitcast.20, f32[2,7168]{1,0:T(2,128)} %refs_3_.5, ...), custom_call_target="tpu_custom_call" | custom-call | tf_op jit(solution)/shard_map/layer_sent/pallas_call | solution.py:127
  62.5 2.4 %collective-permute-start.9 = (bf16[64,3584]{1,0:T(8,128)(2,1)}, bf16[64,3584]{1,0:T(8,128)(2,1)S(1)}, u32[]{:S(2)}, u32[]{:S(2)}) collective-permute-start(bf16[64,3584]{1,0:T(8,128)(2,1)} %get-tuple-element.39), channel_id=1, source_target_pairs={{0,3},{1,0},{2,1},{3,2},{32,35},{33,32},{34,33},{35,34},{4,7},{5,4... | collective-permute-start | bytes 1376264 | tf_op jit(solution)/shard_map/ppermute | solution.py:242
  64.9 2.2 %collective-permute-start.8 = (bf16[64,3584]{1,0:T(8,128)(2,1)}, bf16[64,3584]{1,0:T(8,128)(2,1)S(1)}, u32[]{:S(2)}, u32[]{:S(2)}) collective-permute-start(bf16[64,3584]{1,0:T(8,128)(2,1)} %get-tuple-element.38), channel_id=1, source_target_pairs={{0,2},{1,3},{2,0},{3,1},{32,34},{33,35},{34,32},{35,33},{4,6},{5,7... | collective-permute-start | bytes 1376264 | tf_op jit(solution)/shard_map/ppermute | solution.py:242
  67.1 3.6 %collective-permute-start.7 = (bf16[64,3584]{1,0:T(8,128)(2,1)}, bf16[64,3584]{1,0:T(8,128)(2,1)S(1)}, u32[]{:S(2)}, u32[]{:S(2)}) collective-permute-start(bf16[64,3584]{1,0:T(8,128)(2,1)} %get-tuple-element.37), channel_id=1, source_target_pairs={{0,1},{1,2},{2,3},{3,0},{32,33},{33,34},{34,35},{35,32},{4,5},{5,6... | collective-permute-start | bytes 1376264 | tf_op jit(solution)/shard_map/ppermute | solution.py:242
  70.8 0.9 broadcast_in_dim.39
  71.6 18.1 %all_to_all.25 = f32[4,2,7168]{2,1,0:T(2,128)S(1)} all-to-all(f32[4,2,7168]{2,1,0:T(2,128)S(1)} %broadcast_in_dim.39), channel_id=1, replica_groups=mesh['z_hi'=3,'z_lo'=4,'xh'=2,'y'=8,'xl'=2,'core'=2] {'xl','core'}, dimensions={0} | all-to-all | bytes 458752 | tf_op jit(solution)/shard_map/all_to_all | solution.py:184
  89.7 0.1 reduce_sum.36
  89.8 0.1 reshape.108
  89.9 0.0 collective-permute-done.9
  89.9 0.0 collective-permute-done.8
  89.9 0.0 collective-permute-done.7
  90.0 1.5 fusion.13
  91.5 0.1 pad_maximum_fusion
  91.6 0.1 fusion.4
  91.6 27.8 %all_to_all.26 = bf16[16,8,3840]{2,1,0:T(8,128)(2,1)S(1)} all-to-all(bf16[16,8,3840]{2,1,0:T(8,128)(2,1)S(1)} %fusion.4), channel_id=1, replica_groups=mesh['z_hi'=3,'z_lo'=4,'xh'=2,'y'=8,'xl'=2,'core'=2] {'xh','y'}, dimensions={0} | all-to-all | bytes 1966080 | tf_op jit(solution)/shard_map/all_to_all | solution.py:184
  119.5 0.1 convert_reduce_fusion
  119.7 9.9 %all_to_all.27 = bf16[4,8,3840]{2,1,0:T(8,128)(2,1)S(1)} all-to-all(bf16[4,8,3840]{2,1,0:T(8,128)(2,1)S(1)} %broadcast_in_dim.40), channel_id=1, replica_groups=mesh['z_hi'=3,'z_lo'=4,'xh'=2,'y'=8,'xl'=2,'core'=2] {'z_lo'}, dimensions={0} | all-to-all | bytes 491520 | tf_op jit(solution)/shard_map/all_to_all | solution.py:184
  129.6 0.0 copy-start
  129.6 20.0 %all_to_all.28 = bf16[3,8,3840]{2,1,0:T(8,128)(2,1)S(1)} all-to-all(bf16[3,8,3840]{2,1,0:T(8,128)(2,1)S(1)} %broadcast_in_dim.41), channel_id=1, replica_groups=mesh['z_hi'=3,'z_lo'=4,'xh'=2,'y'=8,'xl'=2,'core'=2] {'z_hi'}, dimensions={0} | all-to-all | bytes 368640 | tf_op jit(solution)/shard_map/all_to_all | solution.py:184
  149.8 1.0 broadcast_in_dim.42
  150.8 7.0 %all-to-all-start.4 = ((bf16[16,8,3840]{2,1,0:T(8,128)(2,1)}), bf16[16,8,3840]{2,1,0:T(8,128)(2,1)S(1)}, u32[]{:S(2)}, u32[]{:S(2)}) async-start(bf16[16,8,3840]{2,1,0:T(8,128)(2,1)} %broadcast_in_dim.42), calls=%async_computation.4 | async-start | bytes 1966080 | tf_op jit(solution)/shard_map/all_to_all | solution.py:184
  157.8 0.0 copy-done
  157.8 7.7 %collective-permute-start.6 = (bf16[128,3584]{1,0:T(8,128)(2,1)S(1)}, bf16[128,3584]{1,0:T(8,128)(2,1)S(1)}, u32[]{:S(2)}, u32[]{:S(2)}) collective-permute-start(bf16[128,3584]{1,0:T(8,128)(2,1)S(1)} %copy-done), channel_id=1, source_target_pairs={{0,3},{1,0},{2,1},{3,2},{32,35},{33,32},{34,33},{35,34},{4,7},{5,4... | collective-permute-start | bytes 2752520 | tf_op jit(solution)/shard_map/ppermute | solution.py:244
  165.5 18.4 %collective-permute-done.6 = bf16[128,3584]{1,0:T(8,128)(2,1)S(1)} collective-permute-done((bf16[128,3584]{1,0:T(8,128)(2,1)S(1)}, bf16[128,3584]{1,0:T(8,128)(2,1)S(1)}, u32[]{:S(2)}, u32[]{:S(2)}) %collective-permute-start.6) | collective-permute-done | bytes 917536 | tf_op jit(solution)/shard_map/ppermute | solution.py:244
  183.9 0.0 all-to-all-done.4
  183.9 0.1 convert_element_type.53
  184.1 1.5 slice_multiply_fusion
  185.5 0.8 reshape.110
  186.3 0.9 copy.13
  (15 shorter events, 0.2 us)
Async XLA Ops:
  3.1 29.3 %collective-permute-start = (bf16[32,10880]{1,0:T(8,128)(2,1)}, bf16[32,10880]{1,0:T(8,128)(2,1)}, u32[]{:S(2)}, u32[]{:S(2)}) collective-permute-start(bf16[32,10880]{1,0:T(8,128)(2,1)} %get-tuple-element.25), channel_id=1, source_target_pairs={{1,0},{2,1},{3,2},{0,3},{33,32},{34,33},{35,34},{32,35},{5,4},{6,5... | collective-permute-start | bytes 2088968 | tf_op jit(solution)/shard_map/ppermute | solution.py:229
  15.5 25.8 %collective-permute-start.1 = (bf16[32,10880]{1,0:T(8,128)(2,1)}, bf16[32,10880]{1,0:T(8,128)(2,1)}, u32[]{:S(2)}, u32[]{:S(2)}) collective-permute-start(bf16[32,10880]{1,0:T(8,128)(2,1)} %get-tuple-element.26), channel_id=1, source_target_pairs={{1,0},{34,1},{3,2},{32,3},{33,32},{2,33},{35,34},{0,35},{5,4},{38,... | collective-permute-start | bytes 2088968 | tf_op jit(solution)/shard_map/ppermute | solution.py:229
  19.8 28.5 %collective-permute-start.2 = (bf16[32,10880]{1,0:T(8,128)(2,1)}, bf16[32,10880]{1,0:T(8,128)(2,1)}, u32[]{:S(2)}, u32[]{:S(2)}) collective-permute-start(bf16[32,10880]{1,0:T(8,128)(2,1)} %get-tuple-element.29), channel_id=1, source_target_pairs={{2,0},{3,1},{0,2},{1,3},{34,32},{35,33},{32,34},{33,35},{6,4},{7,5... | collective-permute-start | bytes 2088968 | tf_op jit(solution)/shard_map/ppermute | solution.py:229
  21.7 26.6 %collective-permute-start.3 = (bf16[32,10880]{1,0:T(8,128)(2,1)}, bf16[32,10880]{1,0:T(8,128)(2,1)}, u32[]{:S(2)}, u32[]{:S(2)}) collective-permute-start(bf16[32,10880]{1,0:T(8,128)(2,1)} %get-tuple-element.30), channel_id=1, source_target_pairs={{34,0},{35,1},{32,2},{33,3},{2,32},{3,33},{0,34},{1,35},{38,4},{39... | collective-permute-start | bytes 2088968 | tf_op jit(solution)/shard_map/ppermute | solution.py:229
  26.1 29.3 %collective-permute-start.4 = (bf16[32,10880]{1,0:T(8,128)(2,1)}, bf16[32,10880]{1,0:T(8,128)(2,1)}, u32[]{:S(2)}, u32[]{:S(2)}) collective-permute-start(bf16[32,10880]{1,0:T(8,128)(2,1)} %get-tuple-element.33), channel_id=1, source_target_pairs={{3,0},{0,1},{1,2},{2,3},{35,32},{32,33},{33,34},{34,35},{7,4},{4,5... | collective-permute-start | bytes 2088968 | tf_op jit(solution)/shard_map/ppermute | solution.py:229
  32.4 23.0 %collective-permute-start.5 = (bf16[32,10880]{1,0:T(8,128)(2,1)}, bf16[32,10880]{1,0:T(8,128)(2,1)}, u32[]{:S(2)}, u32[]{:S(2)}) collective-permute-start(bf16[32,10880]{1,0:T(8,128)(2,1)} %get-tuple-element.34), channel_id=1, source_target_pairs={{35,0},{0,1},{33,2},{2,3},{3,32},{32,33},{1,34},{34,35},{39,4},{4,... | collective-permute-start | bytes 2088968 | tf_op jit(solution)/shard_map/ppermute | solution.py:229
  62.5 27.5 %collective-permute-start.9 = (bf16[64,3584]{1,0:T(8,128)(2,1)}, bf16[64,3584]{1,0:T(8,128)(2,1)S(1)}, u32[]{:S(2)}, u32[]{:S(2)}) collective-permute-start(bf16[64,3584]{1,0:T(8,128)(2,1)} %get-tuple-element.39), channel_id=1, source_target_pairs={{0,3},{1,0},{2,1},{3,2},{32,35},{33,32},{34,33},{35,34},{4,7},{5,4... | collective-permute-start | bytes 1376264 | tf_op jit(solution)/shard_map/ppermute | solution.py:242
  64.9 25.1 %collective-permute-start.8 = (bf16[64,3584]{1,0:T(8,128)(2,1)}, bf16[64,3584]{1,0:T(8,128)(2,1)S(1)}, u32[]{:S(2)}, u32[]{:S(2)}) collective-permute-start(bf16[64,3584]{1,0:T(8,128)(2,1)} %get-tuple-element.38), channel_id=1, source_target_pairs={{0,2},{1,3},{2,0},{3,1},{32,34},{33,35},{34,32},{35,33},{4,6},{5,7... | collective-permute-start | bytes 1376264 | tf_op jit(solution)/shard_map/ppermute | solution.py:242
  67.1 22.8 %collective-permute-start.7 = (bf16[64,3584]{1,0:T(8,128)(2,1)}, bf16[64,3584]{1,0:T(8,128)(2,1)S(1)}, u32[]{:S(2)}, u32[]{:S(2)}) collective-permute-start(bf16[64,3584]{1,0:T(8,128)(2,1)} %get-tuple-element.37), channel_id=1, source_target_pairs={{0,1},{1,2},{2,3},{3,0},{32,33},{33,34},{34,35},{35,32},{4,5},{5,6... | collective-permute-start | bytes 1376264 | tf_op jit(solution)/shard_map/ppermute | solution.py:242
  129.6 28.2 %copy-start = (bf16[128,3584]{1,0:T(8,128)(2,1)S(1)}, bf16[128,3584]{1,0:T(8,128)(2,1)}, u32[]{:S(2)}) copy-start(bf16[128,3584]{1,0:T(8,128)(2,1)} %get-tuple-element.35) | copy-start | bytes 2752516
  150.8 33.2 %all-to-all-start.4 = ((bf16[16,8,3840]{2,1,0:T(8,128)(2,1)}), bf16[16,8,3840]{2,1,0:T(8,128)(2,1)S(1)}, u32[]{:S(2)}, u32[]{:S(2)}) async-start(bf16[16,8,3840]{2,1,0:T(8,128)(2,1)} %broadcast_in_dim.42), calls=%async_computation.4 | async-start | bytes 1966080 | tf_op jit(solution)/shard_map/all_to_all | solution.py:184
  157.8 26.1 %collective-permute-start.6 = (bf16[128,3584]{1,0:T(8,128)(2,1)S(1)}, bf16[128,3584]{1,0:T(8,128)(2,1)S(1)}, u32[]{:S(2)}, u32[]{:S(2)}) collective-permute-start(bf16[128,3584]{1,0:T(8,128)(2,1)S(1)} %copy-done), channel_id=1, source_target_pairs={{0,3},{1,0},{2,1},{3,2},{32,35},{33,32},{34,33},{35,34},{4,7},{5,4... | collective-permute-start | bytes 2752520 | tf_op jit(solution)/shard_map/ppermute | solution.py:244
